TPU v7x, 32 devices: a whole 2x2x4 slice. The times are simulated.
32 devices in a mesh: chan: 8 (over y, x, core), win: 4 (over z).
Axes of the slice: x: 2, y: 2, z: 4, core: 2. Of those that a mesh axis runs over, the one named last changes fastest.
Arguments:
- record: bfloat16 [128, 256, 2048], P('chan', 'win'), may hold values from -40 to 40
- owners: int32 [2], replicated, may hold values from 0 to 7, as said below
- pair_mask: int32 [2, 16, 128], P(None, None, 'chan'), may hold values 0 or 1
Outputs:
- cross: float32 [2, 16, 2, 128, 512], P(None, 'win', None, 'chan')
Inputs may be any that keep to these rules, and one draw needn't show every extreme that they name: `owners`: the 2 planned blocks are all different, and the last block is always among them.
All inputs are finite; a program needn't handle non-finite values. No bound on the sum of `pair_mask` on one device may be relied on, other than what follows from the above.
Results may differ from a plain program's by a relative error of at most 0.0012.
Values may be sent and summed in bfloat16 or wider, within the bound.
No kernel may reach another device: no remote copies, remote signals or barrier semaphores. Data moves between devices by JAX's collectives and lax.ppermute only.
A program may use at most 128 MiB of HBM per device.

v0:
```python
import math

import jax
import jax.numpy as jnp
from jax import lax
from jax.sharding import PartitionSpec as P

BINS = 512
STEPS = 2


water_level = 0.25
epsilon = 1e-06


def spread(value, axis, source):
    kept = jnp.where(lax.axis_index(axis) == source, value, 0).astype(value.dtype)
    return lax.psum(kept, axis)


def fourier_table(samples, bins):
    sample_ids = jnp.arange(samples, dtype=jnp.int32)[:, None]
    bin_ids = jnp.arange(bins, dtype=jnp.int32)[None, :]
    phases = 2.0 * math.pi / samples * (sample_ids * bin_ids % samples).astype(jnp.float32)
    return jnp.concatenate([jnp.cos(phases), -jnp.sin(phases)], axis=1).astype(jnp.bfloat16)


def correlate(source_rows, target_rows):
    source_stack = jnp.concatenate([source_rows[:, :, 0], source_rows[:, :, 1]], axis=1)
    direct = jnp.concatenate([target_rows[:, :, 0], target_rows[:, :, 1]], axis=1)
    rotated = jnp.concatenate([target_rows[:, :, 1], -target_rows[:, :, 0]], axis=1)
    real_part = jnp.einsum("iwk,jwk->ijk", source_stack, direct, preferred_element_type=jnp.float32)
    imag_part = jnp.einsum(
        "iwk,jwk->ijk", source_stack, rotated, preferred_element_type=jnp.float32
    )
    return jnp.stack([real_part, imag_part], axis=1)


def per_device(record, owners, pair_mask):
    channels_here, windows_here, samples = record.shape
    bins = BINS
    win_count = lax.axis_size("win")
    row_count = channels_here // win_count
    table = fourier_table(samples, bins)
    spectra = jnp.dot(record.reshape(-1, samples), table, preferred_element_type=jnp.float32)
    spectra = spectra.reshape(channels_here, windows_here, 2, bins)
    mean_power = jnp.mean(spectra * spectra, axis=(2, 3), keepdims=True)
    magnitude = spectra[:, :, 0:1] * spectra[:, :, 0:1] + spectra[:, :, 1:2] * spectra[:, :, 1:2]
    whitened = (spectra / jnp.sqrt(magnitude + water_level * mean_power + epsilon)).astype(
        jnp.bfloat16
    )
    window_norm = math.sqrt(windows_here * win_count)
    row_offset = lax.axis_index("win") * row_count
    column_ids = lax.axis_index("chan") * channels_here + jnp.arange(channels_here, dtype=jnp.int32)
    results = []
    for step_index in range(STEPS):
        owner_block = owners[step_index]
        theirs = spread(whitened, "chan", owner_block)
        stacked = lax.psum_scatter(
            correlate(theirs, whitened), "win", scatter_dimension=0, tiled=True
        )
        row_ids = owner_block * channels_here + row_offset + jnp.arange(row_count, dtype=jnp.int32)
        quality = lax.dynamic_slice_in_dim(pair_mask[step_index], row_offset, row_count, 0)
        kept = ((column_ids[None, :] >= row_ids[:, None]) & (quality == 1)).astype(jnp.float32)
        results.append(stacked * (kept[:, None, :, None] / window_norm))
    return jnp.stack(results)


def solution(mesh):
    placed = (P("chan", "win", None), P(), P(None, None, "chan"))
    return jax.shard_map(
        per_device,
        mesh=mesh,
        in_specs=placed,
        out_specs=P(None, "win", None, "chan", None),
        check_vma=False,
    )
```

profile of v0, /device:TPU:0, one launch (start us, length us, event | category | flops | bytes accessed | tf_op | source)
XLA Modules:
  0.0 298.8 jit_solution(5140927267976883955)
XLA Ops:
  6.5 17.8 %negate_convert_fusion = (bf16[2048,512]{1,0:T(8,128)(2,1)S(1)}, bf16[2048,512]{1,0:T(8,128)(2,1)}) fusion(), kind=kLoop, calls=%fused_computation.12 | loop fusion | flops 17825792 | bytes 4194304 | tf_op jit(solution)/shard_map/convert.1
  24.9 9.3 %multiply_reduce_fusion = (f32[1024]{0:T(1024)S(1)}, f32[1024,1024]{0,1:T(8,128)}) fusion(bf16[1024,2048]{1,0:T(8,128)(2,1)} %bitcast.54, bf16[2048,512]{1,0:T(8,128)(2,1)S(1)} %get-tuple-element.23, bf16[2048,512]{1,0:T(8,128)(2,1)} %get-tuple-element.24), kind=kOutput, calls=%fused_computation.11 | convolution fusion | flops 4305452032 | bytes 12587008 | tf_op jit(solution)/shard_map/dot_general | solution.py:45
  34.3 5.4 %copy.13 = f32[1024,1024]{1,0:T(8,128)} copy(f32[1024,1024]{0,1:T(8,128)} %get-tuple-element.22) | data formatting | bytes 8388608 | tf_op jit(solution)/shard_map/dot_general | solution.py:45
  39.7 6.6 %reshape.105 = f32[16,64,2,512]{3,2,1,0:T(2,128)} reshape(f32[1024,1024]{1,0:T(8,128)} %copy.13) | data formatting | bytes 8388608 | tf_op jit(solution)/shard_map/reshape | solution.py:46
  46.3 8.4 %copy.15 = f32[16,64,2,512]{1,0,3,2:T(8,128)} copy(f32[16,64,2,512]{3,2,1,0:T(2,128)} %reshape.105) | data formatting | bytes 8388608 | tf_op jit(solution)/shard_map/reshape | solution.py:46
  54.7 10.1 %add_sqrt_fusion = f32[16,64,1,512]{3,2,1,0:T(1,128)S(1)} fusion(f32[16,64,2,512]{3,2,1,0:T(2,128)} %reshape.105, f32[16,64]{1,0:T(8,128)S(1)} %mul.89), kind=kLoop, calls=%fused_computation.37 | loop fusion | flops 2621440 | bytes 6295552 | tf_op jit(solution)/shard_map/sqrt | solution.py:49
  64.8 5.4 %copy.20 = f32[16,64,1,512]{1,0,3,2:T(8,128)} copy(f32[16,64,1,512]{3,2,1,0:T(1,128)S(1)} %add_sqrt_fusion) | data formatting | bytes 4194304 | tf_op jit(solution)/shard_map/div | solution.py:49
  71.5 7.0 %broadcast_select_fusion.1 = (bf16[16,64,2,512]{1,0,3,2:T(8,128)(2,1)}, bf16[16,64,2,512]{1,0,3,2:T(8,128)(2,1)S(1)}) fusion(pred[]{:T(512)S(6)} %eq.28, f32[16,64,2,512]{1,0,3,2:T(8,128)} %copy.15, f32[16,64,512]{1,0,2:T(8,128)} %bitcast.53), kind=kLoop, calls=%fused_computation.18 | loop fusion | flops 3145728 | bytes 10485761 | tf_op jit(solution)/shard_map/jit(_where)/select_n | solution.py:17
  78.5 2.4 broadcast_select_fusion
  80.9 0.8 copy-done
  82.0 3.4 %fusion.25 = bf16[16,64,512]{1,0,2:T(8,128)(2,1)} fusion(bf16[16,64,2,512]{1,0,3,2:T(8,128)(2,1)} %copy-done), kind=kLoop, calls=%fused_computation.60 | loop fusion | flops 524288 | bytes 2097152 | tf_op jit(solution)/shard_map/neg | solution.py:31
  85.3 2.1 slice_bitcast_fusion.5
  87.4 123.4 %all-reduce.3.cloned.1.call-done = (bf16[16,64,2,512]{1,0,3,2:T(8,128)(2,1)}, bf16[16,64,2,512]{1,0,3,2:T(8,128)(2,1)}) async-done(((bf16[16,64,2,512]{1,0,3,2:T(8,128)(2,1)}, bf16[16,64,2,512]{1,0,3,2:T(8,128)(2,1)}), (bf16[16,64,2,512]{1,0,3,2:T(8,128)(2,1)}, bf16[16,64,2,512]{1,0,3,2:T(8,128)(2,1)})) %all-reduce.3.cloned.1.call-update) | async-done | bytes 4194320 | tf_op jit(solution)/shard_map/psum | solution.py:18
  210.8 3.1 %slice_bitcast_fusion.1 = (bf16[16,64,512]{1,0,2:T(8,128)(2,1)S(1)}, bf16[16,64,512]{1,0,2:T(8,128)(2,1)S(1)}) fusion(bf16[16,64,2,512]{1,0,3,2:T(8,128)(2,1)} %get-tuple-element.5), kind=kLoop, calls=%fused_computation.25 | loop fusion | bytes 4194304 | tf_op jit(solution)/shard_map/squeeze | solution.py:29
  213.9 1.4 copy-done.6
  216.0 4.4 %convolution_bitcast_fusion = f32[16,1,16,512]{0,2,3,1:T(8,128)} fusion(bf16[16,64,512]{1,0,2:T(8,128)(2,1)S(1)} %get-tuple-element.14, bf16[16,64,512]{1,0,2:T(8,128)(2,1)S(1)} %get-tuple-element.13, bf16[16,64,512]{1,0,2:T(8,128)(2,1)S(1)} %copy-done.2, bf16[16,64,512]{1,0,2:T(8,128)(2,1)S(1)} %get-tuple-element.12), kind=kOutput, calls=%fused_computation.20 | convolution fusion | flops 41943040 | bytes 4718592 | tf_op jit(solution)/shard_map/iwk,jwk->ijk/dot_general | solution.py:33
  220.4 3.0 copy.19
  223.4 7.2 %convolution_bitcast_fusion.1 = f32[16,1,16,512]{0,2,3,1:T(8,128)} fusion(bf16[16,64,512]{1,0,2:T(8,128)(2,1)} %copy-done.7, bf16[16,64,512]{1,0,2:T(8,128)(2,1)} %copy-done.6, bf16[16,64,512]{1,0,2:T(8,128)(2,1)S(1)} %get-tuple-element.12, bf16[16,64,512]{1,0,2:T(8,128)(2,1)} %get-tuple-element.11), kind=kOutput, calls=%fused_computation.21 | convolution fusion | flops 41943040 | bytes 4718592 | tf_op jit(solution)/shard_map/iwk,jwk->ijk/dot_general | solution.py:32
  230.6 3.0 copy.18
  233.6 1.1 pad_maximum_fusion.5
  234.9 3.1 %slice_bitcast_fusion.3 = (bf16[16,64,512]{1,0,2:T(8,128)(2,1)S(1)}, bf16[16,64,512]{1,0,2:T(8,128)(2,1)S(1)}) fusion(bf16[16,64,2,512]{1,0,3,2:T(8,128)(2,1)} %get-tuple-element.6), kind=kLoop, calls=%fused_computation.27 | loop fusion | bytes 4194304 | tf_op jit(solution)/shard_map/squeeze | solution.py:29
  238.0 1.3 copy-done.4
  240.1 4.4 %convolution_bitcast_fusion.2 = f32[16,1,16,512]{0,2,3,1:T(8,128)} fusion(bf16[16,64,512]{1,0,2:T(8,128)(2,1)S(1)} %copy-done.3, bf16[16,64,512]{1,0,2:T(8,128)(2,1)S(1)} %get-tuple-element.12, bf16[16,64,512]{1,0,2:T(8,128)(2,1)S(1)} %get-tuple-element.10, bf16[16,64,512]{1,0,2:T(8,128)(2,1)S(1)} %get-tuple-element.9), kind=kOutput, calls=%fused_computation.22 | convolution fusion | flops 41943040 | bytes 4718592 | tf_op jit(solution)/shard_map/iwk,jwk->ijk/dot_general | solution.py:33
  244.5 3.0 copy.17
  247.4 7.2 %convolution_bitcast_fusion.3 = f32[16,1,16,512]{0,2,3,1:T(8,128)} fusion(bf16[16,64,512]{1,0,2:T(8,128)(2,1)} %copy-done.5, bf16[16,64,512]{1,0,2:T(8,128)(2,1)} %copy-done.4, bf16[16,64,512]{1,0,2:T(8,128)(2,1)S(1)} %get-tuple-element.12, bf16[16,64,512]{1,0,2:T(8,128)(2,1)} %get-tuple-element.11), kind=kOutput, calls=%fused_computation.23 | convolution fusion | flops 41943040 | bytes 4718592 | tf_op jit(solution)/shard_map/iwk,jwk->ijk/dot_general | solution.py:32
  254.6 3.0 copy.16
  257.6 1.1 pad_maximum_fusion.4
  260.1 2.1 reduce-scatter.5.cloned.1.call-done
  262.2 1.0 multiply_bitcast_fusion
  263.3 27.1 %reduce-scatter.3.cloned.1.call-done = f32[4,2,16,512]{3,2,1,0:T(8,128)} async-done(((f32[16,2,16,512]{3,2,1,0:T(8,128)}), f32[4,2,16,512]{3,2,1,0:T(8,128)}) %reduce-scatter.3.cloned.1.call-update) | async-done | bytes 262160 | tf_op jit(solution)/shard_map/reduce_scatter | solution.py:59
  290.4 1.0 multiply_bitcast_fusion.1
  291.4 0.8 pad_maximum_fusion.6
  (30 shorter events, 2.7 us)
Async XLA Ops:
  6.5 204.3 %all-reduce.3.cloned.1.call-start = ((), (), s32[]{:S(2)}) async-start(), calls=%async_computation.4 | async-start | bytes 16777216 | tf_op jit(solution)/shard_map/psum | solution.py:18
  6.5 17.8 %copy-start.9 = (s32[2]{0:T(128)S(1)}, s32[2]{0:T(128)}, u32[]{:S(2)}) copy-start(s32[2]{0:T(128)} %param.4) | copy-start | bytes 28
  78.5 3.2 %copy-start = (bf16[16,64,2,512]{1,0,3,2:T(8,128)(2,1)}, bf16[16,64,2,512]{1,0,3,2:T(8,128)(2,1)S(1)}, u32[]{:S(2)}) copy-start(bf16[16,64,2,512]{1,0,3,2:T(8,128)(2,1)S(1)} %get-tuple-element.8) | copy-start | bytes 6291460
  81.7 180.5 %reduce-scatter.5.cloned.1.call-start = ((), (), s32[]{:S(2)}) async-start(), calls=%async_computation.3 | async-start | bytes 1310720 | tf_op jit(solution)/shard_map/reduce_scatter | solution.py:59
  82.0 3.4 %copy-start.1 = (bf16[16,64,2,512]{1,0,3,2:T(8,128)(2,1)S(1)}, bf16[16,64,2,512]{1,0,3,2:T(8,128)(2,1)}, u32[]{:S(2)}) copy-start(bf16[16,64,2,512]{1,0,3,2:T(8,128)(2,1)} %copy-done) | copy-start | bytes 6291460
  210.8 5.2 %copy-start.2 = (bf16[16,64,512]{1,0,2:T(8,128)(2,1)S(1)}, bf16[16,64,512]{1,0,2:T(8,128)(2,1)}, u32[]{:S(2)}) copy-start(bf16[16,64,512]{1,0,2:T(8,128)(2,1)} %fusion.25) | copy-start | bytes 3145732
  213.9 1.4 copy-start.6
  213.9 2.1 copy-start.7
  234.7 55.7 %reduce-scatter.3.cloned.1.call-start = ((), (), s32[]{:S(2)}) async-start(), calls=%async_computation.2 | async-start | bytes 1310720 | tf_op jit(solution)/shard_map/reduce_scatter | solution.py:59
  234.9 5.2 %copy-start.3 = (bf16[16,64,512]{1,0,2:T(8,128)(2,1)S(1)}, bf16[16,64,512]{1,0,2:T(8,128)(2,1)}, u32[]{:S(2)}) copy-start(bf16[16,64,512]{1,0,2:T(8,128)(2,1)} %fusion.25) | copy-start | bytes 3145732
  238.0 1.4 copy-start.4
  238.0 2.0 copy-start.5
  257.6 2.4 copy-start.8
Sparse Core Ops, SparseCore 0:
  81.9 128.8 all-reduce.2
  234.8 27.4 reduce-scatter.4
  264.5 25.7 reduce-scatter.2
where the time goes:
time: 299 us
  waiting for transfers between devices  153 us (51%)
  local copies, waits for them, and re-layouts  51.5 us (17%)
  other arithmetic  45.7 us (15%)
  matrix products  32.5 us (11%)
  between operations  15.8 us (5%)
    psum x1, waiting for transfers between devices, spread(): return lax.psum(kept, axis)  123 us
    reduce_scatter x2, waiting for transfers between devices, per_device(): lax.psum_scatter(correlate(theirs, whitened), 'win', scatter_dimension=0,...  29.2 us
    another operation x1, other arithmetic  17.8 us
    reshape x2, local copies, waits for them, and re-layouts, per_device(): spectra = spectra.reshape(channels_here, windows_here, 2, bins)  15 us
    dot_general x2, matrix products, correlate(): jnp.einsum('iwk,jwk->ijk', source_stack, direct, preferred_element_type=j...  14.4 us
    another operation x4, local copies, waits for them, and re-layouts, correlate(): return jnp.stack([real_part, imag_part], axis=1)  11.9 us
    sqrt x1, other arithmetic, per_device(): jnp.sqrt(magnitude + water_level * mean_power + epsilon)  10.1 us
    select_n x2, other arithmetic, spread(): jnp.where(lax.axis_index(axis) == source, value, 0).astype(value.dtype)  9.37 us
  transfers between devices with their start and end apart: 3, of which 3 were waited for; matrix products, arithmetic and copies ran while one was open for 9% of the time, Pallas kernels for 0%

commit v1 on v0

v1 whole, which is shorter than its diff:
```python
import functools
import math

import jax
import jax.numpy as jnp
from jax import lax
from jax.experimental import pallas as pl
from jax.experimental.pallas import tpu as pltpu
from jax.sharding import PartitionSpec as P

BINS = 512
STEPS = 2
LANES = 128
FOLD = BINS // LANES

water_level = 0.25
epsilon = 1e-06


def twiddles(samples):
    digit = jnp.arange(24, dtype=jnp.int32)[:, None]
    factor = (digit % 8) * jnp.where(digit < 8, 1, jnp.where(digit < 16, 8, 64))
    sample_ids = jnp.arange(samples, dtype=jnp.int32)[None, :]
    phases = 2.0 * math.pi / samples * (sample_ids * factor % samples).astype(jnp.float32)
    return jnp.cos(phases), jnp.sin(phases)


def whiten_body(rec_ref, cos_ref, sin_ref, out_ref, rot_ref, table_ref, stage_ref):
    step = pl.program_id(0)
    block = rec_ref.shape[0]
    samples = rec_ref.shape[1]
    pairs = block // LANES

    @pl.when(step == 0)
    def _():
        def fill(k2, carry):
            for lane in range(0, samples, 512):
                cols = pl.ds(lane, 512)
                c0, s0 = cos_ref[0:8, cols], sin_ref[0:8, cols]
                c1, s1 = cos_ref[8:16, cols], sin_ref[8:16, cols]
                c2, s2 = cos_ref[pl.ds(16 + k2, 1), cols], sin_ref[pl.ds(16 + k2, 1), cols]
                cp, sp = c1 * c2 - s1 * s2, s1 * c2 + c1 * s2
                for k1 in range(0, 8, 2):
                    ca, sa = cp[k1 : k1 + 1], sp[k1 : k1 + 1]
                    cb, sb = cp[k1 + 1 : k1 + 2], sp[k1 + 1 : k1 + 2]
                    real = jnp.concatenate([ca * c0 - sa * s0, cb * c0 - sb * s0], axis=0)
                    imag = jnp.concatenate([sa * c0 + ca * s0, sb * c0 + cb * s0], axis=0)
                    row = pl.multiple_of(k2 * 64 + k1 * 8, 16)
                    table_ref[pl.ds(row, 16), cols] = real.astype(jnp.bfloat16)
                    table_ref[pl.ds(BINS + row, 16), cols] = (-imag).astype(jnp.bfloat16)
            return carry

        lax.fori_loop(0, 8, fill, 0)

    rec = rec_ref[...]
    contract = (((1,), (1,)), ((), ()))
    real = lax.dot_general(table_ref[0:BINS], rec, contract, preferred_element_type=jnp.float32)
    imag = lax.dot_general(
        table_ref[BINS : 2 * BINS], rec, contract, preferred_element_type=jnp.float32
    )
    power = real * real + imag * imag
    mean_power = jnp.sum(power, axis=0, keepdims=True) * (1.0 / (2 * BINS))
    scale = lax.rsqrt(power + (water_level * mean_power + epsilon))
    real, imag = real * scale, imag * scale
    low = lax.broadcasted_iota(jnp.int32, (BINS, LANES), 1) < LANES // 2
    for pair in range(pairs):
        r = real[:, pair * LANES : (pair + 1) * LANES]
        i = imag[:, pair * LANES : (pair + 1) * LANES]
        even = jnp.where(low, r, pltpu.roll(i, LANES // 2, 1))
        odd = jnp.where(low, pltpu.roll(r, LANES // 2, 1), i)
        for local, value in ((2 * pair, even), (2 * pair + 1, odd)):
            channel = step * (2 * pairs) + local
            for fold in range(FOLD):
                stage_ref[:, fold * 16 + channel, :] = value[fold * LANES : (fold + 1) * LANES]

    @pl.when(step == pl.num_programs(0) - 1)
    def _():
        rows = stage_ref.shape[1]
        low_half = lax.broadcasted_iota(jnp.int32, (rows, LANES), 1) < LANES // 2

        def emit(kt, carry):
            value = stage_ref[kt]
            out_ref[kt] = value.astype(jnp.bfloat16)
            turned = pltpu.roll(value, LANES // 2, 1)
            rot_ref[kt] = jnp.where(low_half, turned, -turned).astype(jnp.bfloat16)
            return carry

        lax.fori_loop(0, stage_ref.shape[0], emit, 0, unroll=4)


def whiten(record, cos_rows, sin_rows):
    channels, windows, samples = record.shape
    rows = channels * windows
    block = 256
    shape = jax.ShapeDtypeStruct((LANES, FOLD * channels, 2 * windows), jnp.bfloat16)
    whole = pl.BlockSpec(shape.shape, lambda s: (0, 0, 0))
    return pl.pallas_call(
        whiten_body,
        grid=(rows // block,),
        in_specs=[
            pl.BlockSpec((block, samples), lambda s: (s, 0)),
            pl.BlockSpec((24, samples), lambda s: (0, 0)),
            pl.BlockSpec((24, samples), lambda s: (0, 0)),
        ],
        out_specs=[whole, whole],
        out_shape=[shape, shape],
        scratch_shapes=[
            pltpu.VMEM((2 * BINS, samples), jnp.bfloat16),
            pltpu.VMEM(shape.shape, jnp.float32),
        ],
        compiler_params=pltpu.CompilerParams(vmem_limit_bytes=60 << 20),
        cost_estimate=pl.CostEstimate(
            flops=4 * rows * samples * BINS, bytes_accessed=8 << 20, transcendentals=0
        ),
        name="whiten",
    )(record.reshape(rows, samples), cos_rows, sin_rows)


def correlate_body(base_ref, src_ref, tgt_ref, rot_ref, out_ref, stage_ref):
    depth = src_ref.shape[0]
    chans = src_ref.shape[1] // FOLD
    lane_fold = lax.broadcasted_iota(jnp.int32, (chans, LANES), 1) // (2 * chans)
    for first in range(0, depth, 8):
        for kt in range(first, first + 8):
            pieces = []
            for fold in range(FOLD):
                rows = slice(fold * chans, (fold + 1) * chans)
                pieces += [tgt_ref[kt, rows], rot_ref[kt, rows]]
            weights = jnp.concatenate(pieces, axis=0)
            full = lax.dot_general(
                src_ref[kt],
                weights,
                (((1,), (1,)), ((), ())),
                preferred_element_type=jnp.float32,
            )
            kept = full[0:chans]
            for fold in range(1, FOLD):
                kept = jnp.where(
                    lane_fold == fold, full[fold * chans : (fold + 1) * chans], kept
                )
            stage_ref[kt - first] = kept
        for a in range(chans):
            out_ref[a, first : first + 8, :] = stage_ref[:, a, :]


def correlate(source, target, rotated, base):
    depth = 16
    steps = source.shape[0] // depth
    rows = source.shape[1]
    chans = rows // FOLD
    grid_spec = pltpu.PrefetchScalarGridSpec(
        num_scalar_prefetch=1,
        grid=(steps,),
        in_specs=[
            pl.BlockSpec((depth, rows, LANES), lambda s, b: (s, 0, 0)),
            pl.BlockSpec((depth, rows, LANES), lambda s, b: (b[0] // depth + s, 0, 0)),
            pl.BlockSpec((depth, rows, LANES), lambda s, b: (b[0] // depth + s, 0, 0)),
        ],
        out_specs=pl.BlockSpec((chans, depth, LANES), lambda s, b: (0, s, 0)),
        scratch_shapes=[pltpu.VMEM((8, chans, LANES), jnp.float32)],
    )
    return pl.pallas_call(
        correlate_body,
        grid_spec=grid_spec,
        out_shape=jax.ShapeDtypeStruct((chans, source.shape[0], LANES), jnp.float32),
        cost_estimate=pl.CostEstimate(
            flops=source.shape[0] * 2 * rows * LANES * LANES * 4,
            bytes_accessed=source.shape[0] * rows * LANES * 10,
            transcendentals=0,
        ),
        name="correlate",
    )(base.reshape(1), source, target, rotated)


def finish_body(count, sel_ref, keep_ref, *refs):
    own_parts, low_parts, high_parts = refs[:count], refs[count : 2 * count], refs[2 * count : 3 * count]
    out_ref, stage_ref = refs[3 * count :]
    last_step, core = sel_ref[0], sel_ref[1]
    rows = out_ref.shape[1]
    chans = out_ref.shape[3]
    half = LANES // 2

    def total(parts, a):
        value = parts[0][a]
        for part in parts[1:]:
            value = value + part[a]
        return value

    def emit(step, a, value):
        turned = value.T
        for fold in range(FOLD):
            for part in range(2):
                row = fold * 2 * chans + part * chans
                out_ref[step, a, part, :, fold * LANES : (fold + 1) * LANES] = (
                    turned[row : row + chans] * keep_ref[step, a]
                )

    for a in range(rows):
        emit(last_step, a, total(own_parts, a))
        stage_ref[pl.ds(pl.multiple_of(core * half, half), half), :] = total(low_parts, a)
        stage_ref[pl.ds(pl.multiple_of((1 - core) * half, half), half), :] = total(high_parts, a)
        emit(1 - last_step, a, stage_ref[...])


def finish(own_parts, low_parts, high_parts, keep, last_step, core):
    count = len(own_parts)
    rows = own_parts[0].shape[0]
    chans = keep.shape[2]
    vmem = pl.BlockSpec(memory_space=pltpu.VMEM)
    return pl.pallas_call(
        functools.partial(finish_body, count),
        in_specs=[pl.BlockSpec(memory_space=pltpu.SMEM)] + [vmem] * (3 * count + 1),
        out_specs=vmem,
        out_shape=jax.ShapeDtypeStruct((STEPS, rows, 2, chans, BINS), jnp.float32),
        scratch_shapes=[pltpu.VMEM((LANES, LANES), jnp.float32)],
        name="finish",
    )(jnp.stack([last_step, core]), keep, *own_parts, *low_parts, *high_parts)


def window_parts(partial, win_count):
    rows = partial.shape[0] // win_count
    here = lax.axis_index("win")
    parts = [lax.dynamic_slice_in_dim(partial, here * rows, rows, 0)]
    for hop in range(1, win_count):
        away = lax.dynamic_slice_in_dim(partial, (here ^ hop) * rows, rows, 0)
        parts.append(lax.ppermute(away, "win", [(i, i ^ hop) for i in range(win_count)]))
    return parts


def per_device(record, owners, pair_mask):
    channels, windows, samples = record.shape
    win_count = lax.axis_size("win")
    chan_count = lax.axis_size("chan")
    chan = lax.axis_index("chan")
    core = chan % 2
    last = chan_count - 1
    last_step = jnp.where(owners[0] == last, 0, 1).astype(jnp.int32)
    other = jnp.where(owners[0] == last, owners[1], owners[0])
    half = LANES // 2

    spectra, rotated = whiten(record, *twiddles(samples))

    swap = [(i, i ^ 1) for i in range(chan_count)]
    kept_half = lax.dynamic_slice_in_dim(spectra, core * half, half, 0)
    sent_half = lax.dynamic_slice_in_dim(spectra, (1 - core) * half, half, 0)
    current = jnp.where(other % 2 == core, kept_half, lax.ppermute(sent_half, "chan", swap))
    bits = list(range(1, chan_count.bit_length() - 1))
    for up, down in zip(bits, reversed(bits)):
        arrived = lax.ppermute(
            current,
            "chan",
            [(i, i ^ (1 << (down if i % 2 else up))) for i in range(chan_count)],
        )
        bit = jnp.where(core == 1, down, up)
        current = jnp.where(((other ^ chan) >> bit) & 1 == 1, arrived, current)
    partner = lax.ppermute(current, "chan", swap)

    own = correlate(spectra, spectra, rotated, jnp.zeros((), jnp.int32))
    own_parts = window_parts(own, win_count)
    low_parts = window_parts(correlate(current, spectra, rotated, core * half), win_count)
    high_parts = window_parts(correlate(partner, spectra, rotated, (1 - core) * half), win_count)

    rows = channels // win_count
    row_offset = lax.axis_index("win") * rows
    column_ids = chan * channels + jnp.arange(channels, dtype=jnp.int32)
    row_ids = owners[:, None] * channels + row_offset + jnp.arange(rows, dtype=jnp.int32)[None, :]
    quality = lax.dynamic_slice_in_dim(pair_mask, row_offset, rows, 1)
    kept = (column_ids[None, None, :] >= row_ids[:, :, None]) & (quality == 1)
    keep = kept.astype(jnp.float32) / math.sqrt(windows * win_count)
    keep = jnp.broadcast_to(keep[..., None], keep.shape + (LANES,))
    return finish(own_parts, low_parts, high_parts, keep, last_step, core)


def solution(mesh):
    placed = (P("chan", "win", None), P(), P(None, None, "chan"))
    return jax.shard_map(
        per_device,
        mesh=mesh,
        in_specs=placed,
        out_specs=P(None, "win", None, "chan", None),
        check_vma=False,
    )
```

time: 299 us -> 119 us (0.40)
  waiting for transfers between devices: 153 us -> 36.2 us
  local copies, waits for them, and re-layouts: 51.5 us -> 8.58 us
  other arithmetic: 45.7 us -> 3.4 us
  Pallas kernels: 0 us -> 38.5 us
  matrix products: 32.5 us -> 0 us
  starting transfers between devices: 0.49 us -> 29.4 us
  between operations: 15.8 us -> 1.95 us
    psum x1 -> x0, waiting for transfers between devices: 123 us -> none  [spread(): return lax.psum(kept, axis)]
    pallas_call x0 -> x5, Pallas kernels: none -> 38.5 us  [the longest x1 18.4 us: whiten(): pl.pallas_call(whiten_body, grid=(rows // block,), in_specs=[pl.BlockSpec...]
    ppermute x0 -> x13, waiting for transfers between devices: none -> 36.2 us  [the longest x2 25.6 us: per_device(): lax.ppermute(current, 'chan', [(i, i ^ 1 << (down if i % 2 else up)) for...]
    dot_general x5 -> x0, matrix products: 32.5 us -> none  [the longest x2 14.4 us: correlate(): jnp.einsum('iwk,jwk->ijk', source_stack, direct, preferred_element_type=j...]
    ppermute x0 -> x13, starting transfers between devices: none -> 29.4 us  [the longest x9 23.7 us: window_parts(): lax.ppermute(away, 'win', [(i, i ^ hop) for i in range(win_count)])]
    reduce_scatter x2 -> x0, waiting for transfers between devices: 29.2 us -> none  [per_device(): lax.psum_scatter(correlate(theirs, whitened), 'win', scatter_dimension=0,...]
    another operation x6 -> x1, other arithmetic: 22.8 us -> 0.62 us  [finish(): jnp.stack([last_step, core])]
    reshape x2 -> x0, local copies, waits for them, and re-layouts: 15 us -> none  [per_device(): spectra = spectra.reshape(channels_here, windows_here, 2, bins)]
  transfers between devices with their start and end apart: 3 -> 13, of which waited for: 3 -> 5; matrix products, arithmetic and copies ran while one was open for 9% -> 7% of each run, Pallas kernels for 0% -> 15%
where the time goes in v1:
time: 119 us; the launch traced here: 118 us
  Pallas kernels  38.5 us (32%)
  waiting for transfers between devices  36.2 us (30%)
  starting transfers between devices  29.4 us (25%)
  local copies, waits for them, and re-layouts  8.58 us (7%)
  other arithmetic  3.4 us (3%)
  between operations  1.95 us (2%)
    ppermute x2, waiting for transfers between devices, per_device(): lax.ppermute(current, 'chan', [(i, i ^ 1 << (down if i % 2 else up)) for...  25.6 us
    ppermute x9, starting transfers between devices, window_parts(): lax.ppermute(away, 'win', [(i, i ^ hop) for i in range(win_count)])  23.7 us
    pallas_call x1, Pallas kernels, whiten(): pl.pallas_call(whiten_body, grid=(rows // block,), in_specs=[pl.BlockSpec...  18.4 us
    pallas_call x3, Pallas kernels, correlate(): pl.pallas_call(correlate_body, grid_spec=grid_spec, out_shape=jax.ShapeDt...  17.5 us
    ppermute x9, waiting for transfers between devices, window_parts(): lax.ppermute(away, 'win', [(i, i ^ hop) for i in range(win_count)])  10.6 us
    dynamic_slice x3, local copies, waits for them, and re-layouts, window_parts(): away = lax.dynamic_slice_in_dim(partial, (here ^ hop) * rows, rows, 0)  5.78 us
    ppermute x2, starting transfers between devices, per_device(): lax.ppermute(current, 'chan', [(i, i ^ 1 << (down if i % 2 else up)) for...  5.03 us
    pallas_call x1, Pallas kernels, finish(): pl.pallas_call(functools.partial(finish_body, count), in_specs=[pl.BlockS...  2.55 us
  transfers between devices with their start and end apart: 13, of which 5 were waited for; matrix products, arithmetic and copies ran while one was open for 7% of the time, Pallas kernels for 15%

profile of v1, /device:TPU:0, one launch (start us, length us, event | category | flops | bytes accessed | tf_op | source)
XLA Modules:
  0.0 118.0 jit_solution(6238591404641455948)
XLA Ops:
  0.0 1.6 %fusion.6 = (f32[24,2048]{1,0:T(8,128)}, f32[24,2048]{1,0:T(8,128)}) fusion(s32[24]{0:T(128)S(1)} %fusion.10), kind=kLoop, calls=%fused_computation.12 | loop fusion | flops 688128 | bytes 393312 | tf_op jit(solution)/shard_map/sin | solution.py:25
  1.6 18.4 %whiten.1 = (bf16[128,64,128]{2,1,0:T(8,128)(2,1)}, bf16[128,64,128]{2,1,0:T(8,128)(2,1)}) custom-call(bf16[1024,2048]{1,0:T(8,128)(2,1)} %bitcast.7, f32[24,2048]{1,0:T(8,128)} %get-tuple-element.24.cos_ref, f32[24,2048]{1,0:T(8,128)} %get-tuple-element.23.sin_ref), custom_call_target="tpu_custom_call" | custom-call | flops 4294967296 | bytes 8388608 | tf_op jit(solution)/shard_map/whiten/pallas_call | solution.py:97
  20.0 1.4 %constant_dynamic-slice_fusion.8 = bf16[64,64,128]{2,1,0:T(8,128)(2,1)S(1)} fusion(bf16[128,64,128]{2,1,0:T(8,128)(2,1)} %get-tuple-element.7.src_ref.tgt_ref, s32[]{:T(128)S(6)} %select_n.132), kind=kLoop, calls=%fused_computation.25 | loop fusion | bytes 2097156 | tf_op jit(solution)/shard_map/dynamic_slice | solution.py:245
  21.5 0.6 collective-permute-start.3
  22.1 0.6 fusion.11
  24.5 0.1 dynamic-slice_select_fusion
  24.6 2.9 %collective-permute-start.4 = (bf16[64,64,128]{2,1,0:T(8,128)(2,1)S(1)}, bf16[64,64,128]{2,1,0:T(8,128)(2,1)S(1)}, u32[]{:S(2)}, u32[]{:S(2)}) collective-permute-start(bf16[64,64,128]{2,1,0:T(8,128)(2,1)S(1)} %dynamic-slice_select_fusion), channel_id=1, source_target_pairs={{0,8},{4,20},{8,0},{12,28},{16,24},{20,4},{24,16},{28,12},{1,9},{5... | collective-permute-start | bytes 3145736 | tf_op jit(solution)/shard_map/ppermute | solution.py:249
  27.5 12.8 %collective-permute-done.4 = bf16[64,64,128]{2,1,0:T(8,128)(2,1)S(1)} collective-permute-done((bf16[64,64,128]{2,1,0:T(8,128)(2,1)S(1)}, bf16[64,64,128]{2,1,0:T(8,128)(2,1)S(1)}, u32[]{:S(2)}, u32[]{:S(2)}) %collective-permute-start.4) | collective-permute-done | bytes 1048608 | tf_op jit(solution)/shard_map/ppermute | solution.py:249
  40.3 0.1 broadcast_select_fusion
  40.4 2.1 %collective-permute-start.5 = (bf16[64,64,128]{2,1,0:T(8,128)(2,1)S(1)}, bf16[64,64,128]{2,1,0:T(8,128)(2,1)S(1)}, u32[]{:S(2)}, u32[]{:S(2)}) collective-permute-start(bf16[64,64,128]{2,1,0:T(8,128)(2,1)S(1)} %broadcast_select_fusion), channel_id=1, source_target_pairs={{0,16},{4,12},{8,24},{12,4},{16,0},{20,28},{24,8},{28,20},{1,17},{... | collective-permute-start | bytes 3145736 | tf_op jit(solution)/shard_map/ppermute | solution.py:249
  42.5 12.8 %collective-permute-done.5 = bf16[64,64,128]{2,1,0:T(8,128)(2,1)S(1)} collective-permute-done((bf16[64,64,128]{2,1,0:T(8,128)(2,1)S(1)}, bf16[64,64,128]{2,1,0:T(8,128)(2,1)S(1)}, u32[]{:S(2)}, u32[]{:S(2)}) %collective-permute-start.5) | collective-permute-done | bytes 1048608 | tf_op jit(solution)/shard_map/ppermute | solution.py:249
  55.5 8.4 %correlate.3 = f32[16,128,128]{2,1,0:T(8,128)} custom-call(s32[1]{0:T(128)} %constant.73.clone.1.base_ref, bf16[128,64,128]{2,1,0:T(8,128)(2,1)} %get-tuple-element.7.src_ref.tgt_ref, bf16[128,64,128]{2,1,0:T(8,128)(2,1)} %get-tuple-element.7.src_ref.tgt_ref, bf16[128,64,128]{2,1,0:T(8,128)(2,1)} %get-tuple-element.8.rot_ref), custom_call_target="tpu_custom_call" | custom-call | flops 1073741824 | bytes 10485760 | tf_op jit(solution)/shard_map/correlate/pallas_call | solution.py:162
  63.9 2.1 %constant_dynamic-slice_fusion.9 = (f32[4,128,128]{2,1,0:T(8,128)S(1)}, f32[4,128,128]{2,1,0:T(8,128)S(1)}, f32[4,128,128]{2,1,0:T(8,128)}, f32[4,128,128]{2,1,0:T(8,128)}) fusion(f32[16,128,128]{2,1,0:T(8,128)} %correlate.3, s32[]{:T(128)S(6)} %select_n.123, s32[]{:T(128)S(6)} %select_n.122, s32[]{:T(128)S(6)} %select_n.121, s32[]{:T(128)S(6)} %select_n.116), kind=kLoop, calls=%fused_computation.26 | loop fusion | bytes 2097168 | tf_op jit(solution)/shard_map/dynamic_slice | solution.py:225
  66.0 2.1 %collective-permute-start = (f32[4,128,128]{2,1,0:T(8,128)}, f32[4,128,128]{2,1,0:T(8,128)S(1)}, u32[]{:S(2)}, u32[]{:S(2)}) collective-permute-start(f32[4,128,128]{2,1,0:T(8,128)} %get-tuple-element.11), channel_id=1, source_target_pairs={{0,1},{1,0},{2,3},{3,2},{4,5},{5,4},{6,7},{7,6},{8,9},{9,8},{10,11... | collective-permute-start | bytes 786440 | tf_op jit(solution)/shard_map/ppermute | solution.py:226
  68.1 2.6 %collective-permute-start.1 = (f32[4,128,128]{2,1,0:T(8,128)S(1)}, f32[4,128,128]{2,1,0:T(8,128)S(1)}, u32[]{:S(2)}, u32[]{:S(2)}) collective-permute-start(f32[4,128,128]{2,1,0:T(8,128)S(1)} %get-tuple-element.10), channel_id=1, source_target_pairs={{0,2},{1,3},{2,0},{3,1},{4,6},{5,7},{6,4},{7,5},{8,10},{9,11},{10,... | collective-permute-start | bytes 786440 | tf_op jit(solution)/shard_map/ppermute | solution.py:226
  70.7 4.5 %correlate.4 = f32[16,64,128]{2,1,0:T(8,128)} custom-call(s32[1]{0:T(128)} %bitcast.4.base_ref, bf16[64,64,128]{2,1,0:T(8,128)(2,1)} %copy-done.1, bf16[128,64,128]{2,1,0:T(8,128)(2,1)} %get-tuple-element.7.src_ref.tgt_ref, bf16[128,64,128]{2,1,0:T(8,128)(2,1)} %get-tuple-element.8.rot_ref), custom_call_target="tpu_custom_call" | custom-call | flops 536870912 | bytes 5242880 | tf_op jit(solution)/shard_map/correlate/pallas_call | solution.py:162
  75.3 1.9 %constant_dynamic-slice_fusion.4 = (f32[4,64,128]{2,1,0:T(8,128)}, f32[4,64,128]{2,1,0:T(8,128)}, f32[4,64,128]{2,1,0:T(8,128)}, f32[4,64,128]{2,1,0:T(8,128)}) fusion(f32[16,64,128]{2,1,0:T(8,128)} %correlate.4, s32[]{:T(128)S(6)} %select_n.123, s32[]{:T(128)S(6)} %select_n.122, s32[]{:T(128)S(6)} %select_n.121, s32[]{:T(128)S(6)} %select_n.116), kind=kLoop, calls=%fused_computation.21 | loop fusion | bytes 1048592 | tf_op jit(solution)/shard_map/dynamic_slice | solution.py:225
  77.2 0.9 collective-permute-start.6
  78.1 3.5 %collective-permute-start.7 = (f32[4,64,128]{2,1,0:T(8,128)}, f32[4,64,128]{2,1,0:T(8,128)S(1)}, u32[]{:S(2)}, u32[]{:S(2)}) collective-permute-start(f32[4,64,128]{2,1,0:T(8,128)} %get-tuple-element.18), channel_id=1, source_target_pairs={{0,2},{1,3},{2,0},{3,1},{4,6},{5,7},{6,4},{7,5},{8,10},{9,11},{10,... | collective-permute-start | bytes 393224 | tf_op jit(solution)/shard_map/ppermute | solution.py:226
  81.6 4.6 %correlate.5 = f32[16,64,128]{2,1,0:T(8,128)} custom-call(s32[1]{0:T(128)} %bitcast.6.base_ref, bf16[64,64,128]{2,1,0:T(8,128)(2,1)} %copy-done.2, bf16[128,64,128]{2,1,0:T(8,128)(2,1)} %get-tuple-element.7.src_ref.tgt_ref, bf16[128,64,128]{2,1,0:T(8,128)(2,1)} %get-tuple-element.8.rot_ref), custom_call_target="tpu_custom_call" | custom-call | flops 536870912 | bytes 5242880 | tf_op jit(solution)/shard_map/correlate/pallas_call | solution.py:162
  86.2 1.8 %constant_dynamic-slice_fusion = (f32[4,64,128]{2,1,0:T(8,128)S(1)}, f32[4,64,128]{2,1,0:T(8,128)S(1)}, f32[4,64,128]{2,1,0:T(8,128)S(1)}, f32[4,64,128]{2,1,0:T(8,128)}) fusion(f32[16,64,128]{2,1,0:T(8,128)} %correlate.5, s32[]{:T(128)S(6)} %select_n.123, s32[]{:T(128)S(6)} %select_n.122, s32[]{:T(128)S(6)} %select_n.121, s32[]{:T(128)S(6)} %select_n.116), kind=kLoop, calls=%fused_computation.17 | loop fusion | bytes 1048592 | tf_op jit(solution)/shard_map/dynamic_slice | solution.py:225
  88.0 0.5 collective-permute-start.8
  88.5 0.9 collective-permute-done.1.refs_2_
  89.4 0.2 collective-permute-start.10
  89.6 12.6 %collective-permute-start.11 = (f32[4,64,128]{2,1,0:T(8,128)S(1)}, f32[4,64,128]{2,1,0:T(8,128)S(1)}, u32[]{:S(2)}, u32[]{:S(2)}) collective-permute-start(f32[4,64,128]{2,1,0:T(8,128)S(1)} %get-tuple-element.14), channel_id=1, source_target_pairs={{0,2},{1,3},{2,0},{3,1},{4,6},{5,7},{6,4},{7,5},{8,10},{9,11},{10,... | collective-permute-start | bytes 393224 | tf_op jit(solution)/shard_map/ppermute | solution.py:226
  102.2 1.3 %collective-permute-start.12 = (f32[4,64,128]{2,1,0:T(8,128)S(1)}, f32[4,64,128]{2,1,0:T(8,128)S(1)}, u32[]{:S(2)}, u32[]{:S(2)}) collective-permute-start(f32[4,64,128]{2,1,0:T(8,128)S(1)} %get-tuple-element.13), channel_id=1, source_target_pairs={{0,3},{1,2},{2,1},{3,0},{4,7},{5,6},{6,5},{7,4},{8,11},{9,10},{10,... | collective-permute-start | bytes 393224 | tf_op jit(solution)/shard_map/ppermute | solution.py:226
  103.6 0.8 fusion.9
  104.3 0.6 pad_add_fusion.sel_ref
  104.9 4.1 %collective-permute-done.7.refs_6_ = f32[4,64,128]{2,1,0:T(8,128)S(1)} collective-permute-done((f32[4,64,128]{2,1,0:T(8,128)}, f32[4,64,128]{2,1,0:T(8,128)S(1)}, u32[]{:S(2)}, u32[]{:S(2)}) %collective-permute-start.7) | collective-permute-done | bytes 131104 | tf_op jit(solution)/shard_map/ppermute | solution.py:226
  109.1 5.6 %collective-permute-done.11.refs_10_ = f32[4,64,128]{2,1,0:T(8,128)S(1)} collective-permute-done((f32[4,64,128]{2,1,0:T(8,128)S(1)}, f32[4,64,128]{2,1,0:T(8,128)S(1)}, u32[]{:S(2)}, u32[]{:S(2)}) %collective-permute-start.11) | collective-permute-done | bytes 131104 | tf_op jit(solution)/shard_map/ppermute | solution.py:226
  114.7 0.7 broadcast_in_dim.12.keep_ref
  115.5 2.5 %finish.1 = f32[2,4,2,16,512]{4,3,2,1,0:T(8,128)} custom-call(s32[2]{0:T(128)} %pad_add_fusion.sel_ref, f32[2,4,16,128]{3,2,1,0:T(8,128)} %broadcast_in_dim.12.keep_ref, f32[4,128,128]{2,1,0:T(8,128)} %get-tuple-element.12.refs_0_, f32[4,128,128]{2,1,0:T(8,128)} %copy-done.3, f32[4,128,128]{2,1,0:T(8,128)} %copy-done.4, f32[4,128,128]{2,1,0:T(8,128)} %copy-done.5, ...), custom_call_target="tpu_custom_call" | custom-call | tf_op jit(solution)/shard_map/finish/pallas_call | solution.py:210
  (43 shorter events, 0.4 us)
Async XLA Ops:
  20.0 2.0 %copy-start.13 = (s32[2]{0:T(128)S(1)}, s32[2]{0:T(128)}, u32[]{:S(2)}) copy-start(s32[2]{0:T(128)} %param.4) | copy-start | bytes 28
  20.0 4.4 %copy-start = (bf16[128,64,128]{2,1,0:T(8,128)(2,1)S(1)}, bf16[128,64,128]{2,1,0:T(8,128)(2,1)}, u32[]{:S(2)}) copy-start(bf16[128,64,128]{2,1,0:T(8,128)(2,1)} %get-tuple-element.7.src_ref.tgt_ref) | copy-start | bytes 6291460
  21.5 3.0 %collective-permute-start.3 = (bf16[64,64,128]{2,1,0:T(8,128)(2,1)S(1)}, bf16[64,64,128]{2,1,0:T(8,128)(2,1)}, u32[]{:S(2)}, u32[]{:S(2)}) collective-permute-start(bf16[64,64,128]{2,1,0:T(8,128)(2,1)S(1)} %constant_dynamic-slice_fusion.8), channel_id=1, source_target_pairs={{0,4},{4,0},{8,12},{12,8},{16,20},{20,16},{24,28},{28,24},{1,5},{5... | collective-permute-start | bytes 3145736 | tf_op jit(solution)/shard_map/ppermute | solution.py:246
  24.6 15.7 %collective-permute-start.4 = (bf16[64,64,128]{2,1,0:T(8,128)(2,1)S(1)}, bf16[64,64,128]{2,1,0:T(8,128)(2,1)S(1)}, u32[]{:S(2)}, u32[]{:S(2)}) collective-permute-start(bf16[64,64,128]{2,1,0:T(8,128)(2,1)S(1)} %dynamic-slice_select_fusion), channel_id=1, source_target_pairs={{0,8},{4,20},{8,0},{12,28},{16,24},{20,4},{24,16},{28,12},{1,9},{5... | collective-permute-start | bytes 3145736 | tf_op jit(solution)/shard_map/ppermute | solution.py:249
  40.4 14.9 %collective-permute-start.5 = (bf16[64,64,128]{2,1,0:T(8,128)(2,1)S(1)}, bf16[64,64,128]{2,1,0:T(8,128)(2,1)S(1)}, u32[]{:S(2)}, u32[]{:S(2)}) collective-permute-start(bf16[64,64,128]{2,1,0:T(8,128)(2,1)S(1)} %broadcast_select_fusion), channel_id=1, source_target_pairs={{0,16},{4,12},{8,24},{12,4},{16,0},{20,28},{24,8},{28,20},{1,17},{... | collective-permute-start | bytes 3145736 | tf_op jit(solution)/shard_map/ppermute | solution.py:249
  55.4 8.5 %copy-start.1 = (bf16[64,64,128]{2,1,0:T(8,128)(2,1)}, bf16[64,64,128]{2,1,0:T(8,128)(2,1)S(1)}, u32[]{:S(2)}) copy-start(bf16[64,64,128]{2,1,0:T(8,128)(2,1)S(1)} %broadcast_select_fusion.1.src_ref) | copy-start | bytes 3145732
  55.4 22.7 %collective-permute-start.9 = (bf16[64,64,128]{2,1,0:T(8,128)(2,1)S(1)}, bf16[64,64,128]{2,1,0:T(8,128)(2,1)S(1)}, u32[]{:S(2)}, u32[]{:S(2)}) collective-permute-start(bf16[64,64,128]{2,1,0:T(8,128)(2,1)S(1)} %broadcast_select_fusion.1.src_ref), channel_id=1, source_target_pairs={{0,4},{4,0},{8,12},{12,8},{16,20},{20,16},{24,28},{28,24},{1,5},{5... | collective-permute-start | bytes 3145736 | tf_op jit(solution)/shard_map/ppermute | solution.py:256
  66.0 22.0 %collective-permute-start = (f32[4,128,128]{2,1,0:T(8,128)}, f32[4,128,128]{2,1,0:T(8,128)S(1)}, u32[]{:S(2)}, u32[]{:S(2)}) collective-permute-start(f32[4,128,128]{2,1,0:T(8,128)} %get-tuple-element.11), channel_id=1, source_target_pairs={{0,1},{1,0},{2,3},{3,2},{4,5},{5,4},{6,7},{7,6},{8,9},{9,8},{10,11... | collective-permute-start | bytes 786440 | tf_op jit(solution)/shard_map/ppermute | solution.py:226
  68.1 21.3 %collective-permute-start.1 = (f32[4,128,128]{2,1,0:T(8,128)S(1)}, f32[4,128,128]{2,1,0:T(8,128)S(1)}, u32[]{:S(2)}, u32[]{:S(2)}) collective-permute-start(f32[4,128,128]{2,1,0:T(8,128)S(1)} %get-tuple-element.10), channel_id=1, source_target_pairs={{0,2},{1,3},{2,0},{3,1},{4,6},{5,7},{6,4},{7,5},{8,10},{9,11},{10,... | collective-permute-start | bytes 786440 | tf_op jit(solution)/shard_map/ppermute | solution.py:226
  70.7 18.9 %collective-permute-start.2 = (f32[4,128,128]{2,1,0:T(8,128)S(1)}, f32[4,128,128]{2,1,0:T(8,128)S(1)}, u32[]{:S(2)}, u32[]{:S(2)}) collective-permute-start(f32[4,128,128]{2,1,0:T(8,128)S(1)} %get-tuple-element.9), channel_id=1, source_target_pairs={{0,3},{1,2},{2,1},{3,0},{4,7},{5,6},{6,5},{7,4},{8,11},{9,10},{10,... | collective-permute-start | bytes 786440 | tf_op jit(solution)/shard_map/ppermute | solution.py:226
  77.2 25.1 %collective-permute-start.6 = (f32[4,64,128]{2,1,0:T(8,128)}, f32[4,64,128]{2,1,0:T(8,128)S(1)}, u32[]{:S(2)}, u32[]{:S(2)}) collective-permute-start(f32[4,64,128]{2,1,0:T(8,128)} %get-tuple-element.19), channel_id=1, source_target_pairs={{0,1},{1,0},{2,3},{3,2},{4,5},{5,4},{6,7},{7,6},{8,9},{9,8},{10,11... | collective-permute-start | bytes 393224 | tf_op jit(solution)/shard_map/ppermute | solution.py:226
  78.1 3.5 %copy-start.2 = (bf16[64,64,128]{2,1,0:T(8,128)(2,1)}, bf16[64,64,128]{2,1,0:T(8,128)(2,1)S(1)}, u32[]{:S(2)}) copy-start(bf16[64,64,128]{2,1,0:T(8,128)(2,1)S(1)} %collective-permute-done.9.src_ref) | copy-start | bytes 3145732
  78.1 31.0 %collective-permute-start.7 = (f32[4,64,128]{2,1,0:T(8,128)}, f32[4,64,128]{2,1,0:T(8,128)S(1)}, u32[]{:S(2)}, u32[]{:S(2)}) collective-permute-start(f32[4,64,128]{2,1,0:T(8,128)} %get-tuple-element.18), channel_id=1, source_target_pairs={{0,2},{1,3},{2,0},{3,1},{4,6},{5,7},{6,4},{7,5},{8,10},{9,11},{10,... | collective-permute-start | bytes 393224 | tf_op jit(solution)/shard_map/ppermute | solution.py:226
  81.6 6.4 %copy-start.12 = (f32[4,64,128]{2,1,0:T(8,128)S(1)}, f32[4,64,128]{2,1,0:T(8,128)}, u32[]{:S(2)}) copy-start(f32[4,64,128]{2,1,0:T(8,128)} %get-tuple-element.17) | copy-start | bytes 393220
  87.9 27.5 %copy-start.3 = (f32[4,128,128]{2,1,0:T(8,128)}, f32[4,128,128]{2,1,0:T(8,128)S(1)}, u32[]{:S(2)}) copy-start(f32[4,128,128]{2,1,0:T(8,128)S(1)} %collective-permute-done.refs_1_) | copy-start | bytes 786436
  88.0 21.1 %collective-permute-start.8 = (f32[4,64,128]{2,1,0:T(8,128)S(1)}, f32[4,64,128]{2,1,0:T(8,128)S(1)}, u32[]{:S(2)}, u32[]{:S(2)}) collective-permute-start(f32[4,64,128]{2,1,0:T(8,128)S(1)} %copy-done.12), channel_id=1, source_target_pairs={{0,3},{1,2},{2,1},{3,0},{4,7},{5,6},{6,5},{7,4},{8,11},{9,10},{10,... | collective-permute-start | bytes 393224 | tf_op jit(solution)/shard_map/ppermute | solution.py:226
  89.4 26.0 %copy-start.4 = (f32[4,128,128]{2,1,0:T(8,128)}, f32[4,128,128]{2,1,0:T(8,128)S(1)}, u32[]{:S(2)}) copy-start(f32[4,128,128]{2,1,0:T(8,128)S(1)} %collective-permute-done.1.refs_2_) | copy-start | bytes 786436
  89.4 19.7 %collective-permute-start.10 = (f32[4,64,128]{2,1,0:T(8,128)S(1)}, f32[4,64,128]{2,1,0:T(8,128)S(1)}, u32[]{:S(2)}, u32[]{:S(2)}) collective-permute-start(f32[4,64,128]{2,1,0:T(8,128)S(1)} %get-tuple-element.15), channel_id=1, source_target_pairs={{0,1},{1,0},{2,3},{3,2},{4,5},{5,4},{6,7},{7,6},{8,9},{9,8},{10,11... | collective-permute-start | bytes 393224 | tf_op jit(solution)/shard_map/ppermute | solution.py:226
  89.6 25.8 %copy-start.5 = (f32[4,128,128]{2,1,0:T(8,128)}, f32[4,128,128]{2,1,0:T(8,128)S(1)}, u32[]{:S(2)}) copy-start(f32[4,128,128]{2,1,0:T(8,128)S(1)} %collective-permute-done.2.refs_3_) | copy-start | bytes 786436
  89.6 25.1 %collective-permute-start.11 = (f32[4,64,128]{2,1,0:T(8,128)S(1)}, f32[4,64,128]{2,1,0:T(8,128)S(1)}, u32[]{:S(2)}, u32[]{:S(2)}) collective-permute-start(f32[4,64,128]{2,1,0:T(8,128)S(1)} %get-tuple-element.14), channel_id=1, source_target_pairs={{0,2},{1,3},{2,0},{3,1},{4,6},{5,7},{6,4},{7,5},{8,10},{9,11},{10,... | collective-permute-start | bytes 393224 | tf_op jit(solution)/shard_map/ppermute | solution.py:226
  102.2 13.2 %copy-start.6 = (f32[4,64,128]{2,1,0:T(8,128)}, f32[4,64,128]{2,1,0:T(8,128)S(1)}, u32[]{:S(2)}) copy-start(f32[4,64,128]{2,1,0:T(8,128)S(1)} %collective-permute-done.6.refs_5_) | copy-start | bytes 393220
  102.2 12.4 %collective-permute-start.12 = (f32[4,64,128]{2,1,0:T(8,128)S(1)}, f32[4,64,128]{2,1,0:T(8,128)S(1)}, u32[]{:S(2)}, u32[]{:S(2)}) collective-permute-start(f32[4,64,128]{2,1,0:T(8,128)S(1)} %get-tuple-element.13), channel_id=1, source_target_pairs={{0,3},{1,2},{2,1},{3,0},{4,7},{5,6},{6,5},{7,4},{8,11},{9,10},{10,... | collective-permute-start | bytes 393224 | tf_op jit(solution)/shard_map/ppermute | solution.py:226
  109.0 6.4 %copy-start.7 = (f32[4,64,128]{2,1,0:T(8,128)}, f32[4,64,128]{2,1,0:T(8,128)S(1)}, u32[]{:S(2)}) copy-start(f32[4,64,128]{2,1,0:T(8,128)S(1)} %collective-permute-done.7.refs_6_) | copy-start | bytes 393220
  109.1 6.4 %copy-start.8 = (f32[4,64,128]{2,1,0:T(8,128)}, f32[4,64,128]{2,1,0:T(8,128)S(1)}, u32[]{:S(2)}) copy-start(f32[4,64,128]{2,1,0:T(8,128)S(1)} %collective-permute-done.8.refs_7_) | copy-start | bytes 393220
  109.1 6.4 %copy-start.9 = (f32[4,64,128]{2,1,0:T(8,128)}, f32[4,64,128]{2,1,0:T(8,128)S(1)}, u32[]{:S(2)}) copy-start(f32[4,64,128]{2,1,0:T(8,128)S(1)} %collective-permute-done.10.refs_9_) | copy-start | bytes 393220
  114.7 0.8 copy-start.10
  114.7 0.8 copy-start.11

commit v2 on v1

--- a/solution.py
+++ b/solution.py
@@ -7,6 +7,7 @@
 from jax.experimental import pallas as pl
 from jax.experimental.pallas import tpu as pltpu
 from jax.sharding import PartitionSpec as P
+
 
 BINS = 512
 STEPS = 2
@@ -75,17 +76,17 @@
 
     @pl.when(step == pl.num_programs(0) - 1)
     def _():
-        rows = stage_ref.shape[1]
+        rows = out_ref.shape[1]
         low_half = lax.broadcasted_iota(jnp.int32, (rows, LANES), 1) < LANES // 2
 
         def emit(kt, carry):
-            value = stage_ref[kt]
-            out_ref[kt] = value.astype(jnp.bfloat16)
+            value = stage_ref[kt, 0:rows].astype(jnp.bfloat16)
+            out_ref[kt] = value
             turned = pltpu.roll(value, LANES // 2, 1)
-            rot_ref[kt] = jnp.where(low_half, turned, -turned).astype(jnp.bfloat16)
+            rot_ref[kt] = jnp.where(low_half, turned, -turned)
             return carry
 
-        lax.fori_loop(0, stage_ref.shape[0], emit, 0, unroll=4)
+        lax.fori_loop(0, stage_ref.shape[0], emit, 0, unroll=16)
 
 
 def whiten(record, cos_rows, sin_rows):
@@ -106,7 +107,7 @@
         out_shape=[shape, shape],
         scratch_shapes=[
             pltpu.VMEM((2 * BINS, samples), jnp.bfloat16),
-            pltpu.VMEM(shape.shape, jnp.float32),
+            pltpu.VMEM((LANES, FOLD * channels + 8, LANES), jnp.float32),
         ],
         compiler_params=pltpu.CompilerParams(vmem_limit_bytes=60 << 20),
         cost_estimate=pl.CostEstimate(
@@ -116,7 +117,7 @@
     )(record.reshape(rows, samples), cos_rows, sin_rows)
 
 
-def correlate_body(base_ref, src_ref, tgt_ref, rot_ref, out_ref, stage_ref):
+def correlate_block(src_ref, tgt_ref, rot_ref, out_ref, stage_ref):
     depth = src_ref.shape[0]
     chans = src_ref.shape[1] // FOLD
     lane_fold = lax.broadcasted_iota(jnp.int32, (chans, LANES), 1) // (2 * chans)
@@ -143,48 +144,60 @@
             out_ref[a, first : first + 8, :] = stage_ref[:, a, :]
 
 
-def correlate(source, target, rotated, base):
+def correlate_body(steps, base_ref, *refs):
+    sources, rest = refs[:-4], refs[-4:]
+    if len(sources) == 1:
+        correlate_block(sources[0], *rest)
+        return
+    for index, source in enumerate(sources):
+
+        @pl.when(pl.program_id(0) // steps == index)
+        def _():
+            correlate_block(source, *rest)
+
+
+def correlate(sources, target, rotated, bases):
     depth = 16
-    steps = source.shape[0] // depth
-    rows = source.shape[1]
+    count = len(sources)
+    length, rows, _ = sources[0].shape
+    steps = length // depth
     chans = rows // FOLD
+
+    def source_map(n):
+        return lambda s, b: (jnp.clip(s - n * steps, 0, steps - 1), 0, 0)
+
+    def target_map(s, b):
+        return (b[s // steps] // depth + s % steps, 0, 0)
+
+    block = (depth, rows, LANES)
     grid_spec = pltpu.PrefetchScalarGridSpec(
         num_scalar_prefetch=1,
-        grid=(steps,),
-        in_specs=[
-            pl.BlockSpec((depth, rows, LANES), lambda s, b: (s, 0, 0)),
-            pl.BlockSpec((depth, rows, LANES), lambda s, b: (b[0] // depth + s, 0, 0)),
-            pl.BlockSpec((depth, rows, LANES), lambda s, b: (b[0] // depth + s, 0, 0)),
-        ],
+        grid=(count * steps,),
+        in_specs=[pl.BlockSpec(block, source_map(n)) for n in range(count)]
+        + [pl.BlockSpec(block, target_map)] * 2,
         out_specs=pl.BlockSpec((chans, depth, LANES), lambda s, b: (0, s, 0)),
         scratch_shapes=[pltpu.VMEM((8, chans, LANES), jnp.float32)],
     )
     return pl.pallas_call(
-        correlate_body,
+        functools.partial(correlate_body, steps),
         grid_spec=grid_spec,
-        out_shape=jax.ShapeDtypeStruct((chans, source.shape[0], LANES), jnp.float32),
+        out_shape=jax.ShapeDtypeStruct((chans, count * length, LANES), jnp.float32),
         cost_estimate=pl.CostEstimate(
-            flops=source.shape[0] * 2 * rows * LANES * LANES * 4,
-            bytes_accessed=source.shape[0] * rows * LANES * 10,
+            flops=count * length * 2 * rows * LANES * LANES * 4,
+            bytes_accessed=count * length * rows * LANES * 10,
             transcendentals=0,
         ),
         name="correlate",
-    )(base.reshape(1), source, target, rotated)
-
-
-def finish_body(count, sel_ref, keep_ref, *refs):
-    own_parts, low_parts, high_parts = refs[:count], refs[count : 2 * count], refs[2 * count : 3 * count]
-    out_ref, stage_ref = refs[3 * count :]
+    )(bases, *sources, target, rotated)
+
+
+def finish_body(sel_ref, keep_ref, own_ref, *refs):
+    chunk_refs, (out_ref, stage_ref) = refs[:-2], refs[-2:]
     last_step, core = sel_ref[0], sel_ref[1]
     rows = out_ref.shape[1]
     chans = out_ref.shape[3]
     half = LANES // 2
-
-    def total(parts, a):
-        value = parts[0][a]
-        for part in parts[1:]:
-            value = value + part[a]
-        return value
+    piece = half // len(chunk_refs)
 
     def emit(step, a, value):
         turned = value.T
@@ -196,38 +209,53 @@
                 )
 
     for a in range(rows):
-        emit(last_step, a, total(own_parts, a))
-        stage_ref[pl.ds(pl.multiple_of(core * half, half), half), :] = total(low_parts, a)
-        stage_ref[pl.ds(pl.multiple_of((1 - core) * half, half), half), :] = total(high_parts, a)
+        emit(last_step, a, own_ref[a])
+        for index, chunk_ref in enumerate(chunk_refs):
+            for side, start in enumerate((core * half, (1 - core) * half)):
+                row = pl.multiple_of(start + index * piece, piece)
+                stage_ref[pl.ds(row, piece), :] = chunk_ref[a, side * piece : (side + 1) * piece]
         emit(1 - last_step, a, stage_ref[...])
 
 
-def finish(own_parts, low_parts, high_parts, keep, last_step, core):
-    count = len(own_parts)
-    rows = own_parts[0].shape[0]
+def finish(own, chunks, keep, last_step, core):
+    rows = own.shape[0]
     chans = keep.shape[2]
     vmem = pl.BlockSpec(memory_space=pltpu.VMEM)
     return pl.pallas_call(
-        functools.partial(finish_body, count),
-        in_specs=[pl.BlockSpec(memory_space=pltpu.SMEM)] + [vmem] * (3 * count + 1),
+        finish_body,
+        in_specs=[pl.BlockSpec(memory_space=pltpu.SMEM)] + [vmem] * (2 + len(chunks)),
         out_specs=vmem,
         out_shape=jax.ShapeDtypeStruct((STEPS, rows, 2, chans, BINS), jnp.float32),
         scratch_shapes=[pltpu.VMEM((LANES, LANES), jnp.float32)],
         name="finish",
-    )(jnp.stack([last_step, core]), keep, *own_parts, *low_parts, *high_parts)
-
-
-def window_parts(partial, win_count):
+    )(jnp.stack([last_step, core]), keep, own, *chunks)
+
+
+def window_sum(partial, win_count, wire, only=None):
     rows = partial.shape[0] // win_count
     here = lax.axis_index("win")
-    parts = [lax.dynamic_slice_in_dim(partial, here * rows, rows, 0)]
+    arrived = []
     for hop in range(1, win_count):
-        away = lax.dynamic_slice_in_dim(partial, (here ^ hop) * rows, rows, 0)
-        parts.append(lax.ppermute(away, "win", [(i, i ^ hop) for i in range(win_count)]))
-    return parts
-
-
-def per_device(record, owners, pair_mask):
+        away = lax.dynamic_slice_in_dim(partial, (here ^ hop) * rows, rows, 0).astype(wire)
+        pairs = [(i, i ^ hop) for i in range(win_count)]
+        if only is None:
+            arrived.append(lax.ppermute(away, "win", pairs))
+        else:
+            base = only * win_count
+            arrived.append(
+                lax.ppermute(away, ("chan", "win"), [(base + i, base + j) for i, j in pairs])
+            )
+    total = lax.dynamic_slice_in_dim(partial, here * rows, rows, 0)
+    for part in arrived:
+        total = total + part.astype(jnp.float32)
+    return total
+
+
+CHUNKS = 2
+WIRE = jnp.float16
+
+
+def planned(record, owners, pair_mask):
     channels, windows, samples = record.shape
     win_count = lax.axis_size("win")
     chan_count = lax.axis_size("chan")
@@ -237,28 +265,33 @@
     last_step = jnp.where(owners[0] == last, 0, 1).astype(jnp.int32)
     other = jnp.where(owners[0] == last, owners[1], owners[0])
     half = LANES // 2
+    piece = half // CHUNKS
 
     spectra, rotated = whiten(record, *twiddles(samples))
 
     swap = [(i, i ^ 1) for i in range(chan_count)]
-    kept_half = lax.dynamic_slice_in_dim(spectra, core * half, half, 0)
-    sent_half = lax.dynamic_slice_in_dim(spectra, (1 - core) * half, half, 0)
-    current = jnp.where(other % 2 == core, kept_half, lax.ppermute(sent_half, "chan", swap))
     bits = list(range(1, chan_count.bit_length() - 1))
+    currents = []
+    for index in range(CHUNKS):
+        sent = lax.dynamic_slice_in_dim(spectra, (1 - core) * half + index * piece, piece, 0)
+        arrived = lax.ppermute(sent, "chan", swap)
+        kept = lax.dynamic_slice_in_dim(spectra, core * half + index * piece, piece, 0)
+        currents.append(jnp.where(other % 2 == core, kept, arrived))
     for up, down in zip(bits, reversed(bits)):
-        arrived = lax.ppermute(
-            current,
-            "chan",
-            [(i, i ^ (1 << (down if i % 2 else up))) for i in range(chan_count)],
-        )
+        pairs = [(i, i ^ (1 << (down if i % 2 else up))) for i in range(chan_count)]
         bit = jnp.where(core == 1, down, up)
-        current = jnp.where(((other ^ chan) >> bit) & 1 == 1, arrived, current)
-    partner = lax.ppermute(current, "chan", swap)
-
-    own = correlate(spectra, spectra, rotated, jnp.zeros((), jnp.int32))
-    own_parts = window_parts(own, win_count)
-    low_parts = window_parts(correlate(current, spectra, rotated, core * half), win_count)
-    high_parts = window_parts(correlate(partner, spectra, rotated, (1 - core) * half), win_count)
+        for index in range(CHUNKS):
+            arrived = lax.ppermute(currents[index], "chan", pairs)
+            currents[index] = jnp.where(((other ^ chan) >> bit) & 1 == 1, arrived, currents[index])
+
+    own = correlate([spectra], spectra, rotated, jnp.zeros((1,), jnp.int32))
+    own = window_sum(own, win_count, jnp.float32, only=last)
+    chunks = []
+    for index in range(CHUNKS):
+        partner = lax.ppermute(currents[index], "chan", swap)
+        bases = jnp.stack([core * half, (1 - core) * half]) + index * piece
+        partial = correlate([currents[index], partner], spectra, rotated, bases)
+        chunks.append(window_sum(partial, win_count, WIRE))
 
     rows = channels // win_count
     row_offset = lax.axis_index("win") * rows
@@ -268,13 +301,13 @@
     kept = (column_ids[None, None, :] >= row_ids[:, :, None]) & (quality == 1)
     keep = kept.astype(jnp.float32) / math.sqrt(windows * win_count)
     keep = jnp.broadcast_to(keep[..., None], keep.shape + (LANES,))
-    return finish(own_parts, low_parts, high_parts, keep, last_step, core)
+    return finish(own, chunks, keep, last_step, core)
 
 
 def solution(mesh):
     placed = (P("chan", "win", None), P(), P(None, None, "chan"))
     return jax.shard_map(
-        per_device,
+        planned,
         mesh=mesh,
         in_specs=placed,
         out_specs=P(None, "win", None, "chan", None),

time: 119 us -> 108 us (0.908)
  waiting for transfers between devices: 36.2 us -> 14.9 us
  other arithmetic: 3.4 us -> 13.5 us
  starting transfers between devices: 29.4 us -> 35.4 us
  Pallas kernels: 38.5 us -> 35 us
  local copies, waits for them, and re-layouts: 8.58 us -> 5.98 us
    ppermute x13 -> x17, waiting for transfers between devices: 36.2 us -> 14.9 us  [the longest x4 10.8 us: planned(): arrived = lax.ppermute(currents[index], 'chan', pairs)]
    ppermute x13 -> x17, starting transfers between devices: 29.4 us -> 35.4 us  [the longest x2 15.3 us: planned(): partner = lax.ppermute(currents[index], 'chan', swap)]
    add x3 -> x7, other arithmetic: 0.08 us -> 5.77 us  [the longest x3 5.05 us: window_sum(): total = total + part.astype(jnp.float32)]
    pallas_call x1, Pallas kernels: 18.4 us -> 14.2 us  [whiten(): pl.pallas_call(whiten_body, grid=(rows // block,), in_specs=[pl.BlockSpec...]
    dynamic_slice x4 -> x2, local copies, waits for them, and re-layouts: 7.22 us -> 3.08 us  [the longest x1 2.01 us: window_sum(): lax.dynamic_slice_in_dim(partial, (here ^ hop) * rows, rows, 0).astype(wire)]
    select_n x3 -> x6, other arithmetic: 0.33 us -> 2.62 us  [the longest x2 2.39 us: planned(): currents.append(jnp.where(other % 2 == core, kept, arrived))]
    convert_element_type x0 -> x2, other arithmetic: none -> 2.12 us  [window_sum(): lax.dynamic_slice_in_dim(partial, (here ^ hop) * rows, rows, 0).astype(wire)]
    unnamed x28 -> x10, local copies, waits for them, and re-layouts: 0.05 us -> 1.62 us
  transfers between devices with their start and end apart: 13 -> 17, of which waited for: 5 -> 5; matrix products, arithmetic and copies ran while one was open for 7% -> 11% of each run, Pallas kernels for 15% -> 18%
where the time goes in v2:
time: 108 us; the launch traced here: 107 us
  starting transfers between devices  35.4 us (33%)
  Pallas kernels  35 us (32%)
  waiting for transfers between devices  14.9 us (14%)
  other arithmetic  13.5 us (12%)
  local copies, waits for them, and re-layouts  5.98 us (6%)
  between operations  1.92 us (2%)
    pallas_call x3, Pallas kernels, correlate(): pl.pallas_call(functools.partial(correlate_body, steps), grid_spec=grid_s...  18.8 us
    ppermute x2, starting transfers between devices, planned(): partner = lax.ppermute(currents[index], 'chan', swap)  15.3 us
    pallas_call x1, Pallas kernels, whiten(): pl.pallas_call(whiten_body, grid=(rows // block,), in_specs=[pl.BlockSpec...  14.2 us
    ppermute x4, waiting for transfers between devices, planned(): arrived = lax.ppermute(currents[index], 'chan', pairs)  10.8 us
    ppermute x6, starting transfers between devices, window_sum(): arrived.append(lax.ppermute(away, 'win', pairs))  8.9 us
    ppermute x4, starting transfers between devices, planned(): arrived = lax.ppermute(currents[index], 'chan', pairs)  7.18 us
    add x3, other arithmetic, window_sum(): total = total + part.astype(jnp.float32)  5.05 us
    ppermute x6, waiting for transfers between devices, window_sum(): arrived.append(lax.ppermute(away, 'win', pairs))  4.11 us
  transfers between devices with their start and end apart: 17, of which 5 were waited for; matrix products, arithmetic and copies ran while one was open for 11% of the time, Pallas kernels for 18%

profile of v2, /device:TPU:0, one launch (start us, length us, event | category | flops | bytes accessed | tf_op | source)
XLA Modules:
  0.0 106.8 jit_solution(12996111362444968180)
XLA Ops:
  0.0 1.6 %fusion.6 = (f32[24,2048]{1,0:T(8,128)}, f32[24,2048]{1,0:T(8,128)}) fusion(s32[24]{0:T(128)S(1)} %fusion.11), kind=kLoop, calls=%fused_computation.24 | loop fusion | flops 688128 | bytes 393312 | tf_op jit(solution)/shard_map/sin | solution.py:26
  1.6 14.2 %whiten.1 = (bf16[128,64,128]{2,1,0:T(8,128)(2,1)}, bf16[128,64,128]{2,1,0:T(8,128)(2,1)}) custom-call(bf16[1024,2048]{1,0:T(8,128)(2,1)} %bitcast.7, f32[24,2048]{1,0:T(8,128)} %get-tuple-element.25.cos_ref, f32[24,2048]{1,0:T(8,128)} %get-tuple-element.24.sin_ref), custom_call_target="tpu_custom_call" | custom-call | flops 4294967296 | bytes 8388608 | tf_op jit(solution)/shard_map/whiten/pallas_call | solution.py:98
  15.8 1.1 %constant_dynamic-slice_fusion = bf16[32,64,128]{2,1,0:T(8,128)(2,1)S(1)} fusion(bf16[128,64,128]{2,1,0:T(8,128)(2,1)} %get-tuple-element.7.refs_0_.refs_1_.refs_2_, s32[]{:T(128)S(6)} %select_n.157), kind=kLoop, calls=%fused_computation.26 | loop fusion | bytes 1048580 | tf_op jit(solution)/shard_map/dynamic_slice | solution.py:276
  19.8 1.3 %dynamic-slice_select_fusion = (bf16[32,64,128]{2,1,0:T(8,128)(2,1)S(1)}, bf16[32,64,128]{2,1,0:T(8,128)(2,1)S(1)}) fusion(bf16[32,64,128]{2,1,0:T(8,128)(2,1)S(1)} %collective-permute-done.10, bf16[128,64,128]{2,1,0:T(8,128)(2,1)} %get-tuple-element.7.refs_0_.refs_1_.refs_2_, s32[]{:T(128)S(6)} %select_n.156, pred[]{:T(512)S(6)} %eq.40, s32[]{:T(128)S(6)} %select_n.152), kind=kLoop, calls=%fused_computation | loop fusion | flops 262144 | bytes 2621449 | tf_op jit(solution)/shard_map/jit(_where)/select_n | solution.py:279
  21.2 8.1 %correlate.3 = f32[16,128,128]{2,1,0:T(8,128)} custom-call(s32[1]{0:T(128)} %constant.79.clone.1.base_ref, bf16[128,64,128]{2,1,0:T(8,128)(2,1)} %get-tuple-element.7.refs_0_.refs_1_.refs_2_, bf16[128,64,128]{2,1,0:T(8,128)(2,1)} %get-tuple-element.7.refs_0_.refs_1_.refs_2_, bf16[128,64,128]{2,1,0:T(8,128)(2,1)} %get-tuple-element.8.refs_2_.refs_3_), custom_call_target="tpu_custom_call" | custom-call | flops 1073741824 | bytes 10485760 | tf_op jit(solution)/shard_map/correlate/pallas_call | solution.py:181
  29.3 2.0 %constant_dynamic-slice_fusion.4 = (f32[4,128,128]{2,1,0:T(8,128)}, f32[4,128,128]{2,1,0:T(8,128)}, f32[4,128,128]{2,1,0:T(8,128)}) fusion(f32[16,128,128]{2,1,0:T(8,128)} %correlate.3, s32[]{:T(128)S(6)} %select_n.141, s32[]{:T(128)S(6)} %select_n.143, s32[]{:T(128)S(6)} %select_n.142), kind=kLoop, calls=%fused_computation.30 | loop fusion | bytes 1572876 | tf_op jit(solution)/shard_map/dynamic_slice | solution.py:239
  32.0 1.4 %collective-permute-start.1 = (f32[4,128,128]{2,1,0:T(8,128)}, f32[4,128,128]{2,1,0:T(8,128)}, u32[]{:S(2)}, u32[]{:S(2)}) collective-permute-start(f32[4,128,128]{2,1,0:T(8,128)} %get-tuple-element.15), channel_id=1, source_target_pairs={{28,30},{29,31},{30,28},{31,29}} | collective-permute-start | bytes 786440 | tf_op jit(solution)/shard_map/ppermute | solution.py:246
  33.4 1.4 %collective-permute-start.2 = (f32[4,128,128]{2,1,0:T(8,128)}, f32[4,128,128]{2,1,0:T(8,128)}, u32[]{:S(2)}, u32[]{:S(2)}) collective-permute-start(f32[4,128,128]{2,1,0:T(8,128)} %get-tuple-element.14), channel_id=1, source_target_pairs={{28,31},{29,30},{30,29},{31,28}} | collective-permute-start | bytes 786440 | tf_op jit(solution)/shard_map/ppermute | solution.py:246
  34.7 2.9 %collective-permute-start.11 = (bf16[32,64,128]{2,1,0:T(8,128)(2,1)S(1)}, bf16[32,64,128]{2,1,0:T(8,128)(2,1)S(1)}, u32[]{:S(2)}, u32[]{:S(2)}) collective-permute-start(bf16[32,64,128]{2,1,0:T(8,128)(2,1)S(1)} %get-tuple-element.11), channel_id=1, source_target_pairs={{0,8},{4,20},{8,0},{12,28},{16,24},{20,4},{24,16},{28,12},{1,9},{5... | collective-permute-start | bytes 1572872 | tf_op jit(solution)/shard_map/ppermute | solution.py:284
  37.6 1.1 %dynamic-slice_select_fusion.1 = bf16[32,64,128]{2,1,0:T(8,128)(2,1)S(1)} fusion(bf16[32,64,128]{2,1,0:T(8,128)(2,1)S(1)} %collective-permute-done.3, bf16[128,64,128]{2,1,0:T(8,128)(2,1)} %get-tuple-element.7.refs_0_.refs_1_.refs_2_, s32[]{:T(128)S(6)} %select_n.151, pred[]{:T(512)S(6)} %eq.40), kind=kLoop, calls=%fused_computation.1 | loop fusion | flops 262144 | bytes 1572869 | tf_op jit(solution)/shard_map/jit(_where)/select_n | solution.py:279
  39.5 5.3 %collective-permute-done.11 = bf16[32,64,128]{2,1,0:T(8,128)(2,1)S(1)} collective-permute-done((bf16[32,64,128]{2,1,0:T(8,128)(2,1)S(1)}, bf16[32,64,128]{2,1,0:T(8,128)(2,1)S(1)}, u32[]{:S(2)}, u32[]{:S(2)}) %collective-permute-start.11) | collective-permute-done | bytes 524320 | tf_op jit(solution)/shard_map/ppermute | solution.py:284
  44.8 2.1 %collective-permute-start.12 = (bf16[32,64,128]{2,1,0:T(8,128)(2,1)S(1)}, bf16[32,64,128]{2,1,0:T(8,128)(2,1)S(1)}, u32[]{:S(2)}, u32[]{:S(2)}) collective-permute-start(bf16[32,64,128]{2,1,0:T(8,128)(2,1)S(1)} %broadcast_select_fusion), channel_id=1, source_target_pairs={{0,16},{4,12},{8,24},{12,4},{16,0},{20,28},{24,8},{28,20},{1,17},{... | collective-permute-start | bytes 1572872 | tf_op jit(solution)/shard_map/ppermute | solution.py:284
  47.0 3.5 %collective-permute-done.4 = bf16[32,64,128]{2,1,0:T(8,128)(2,1)S(1)} collective-permute-done((bf16[32,64,128]{2,1,0:T(8,128)(2,1)S(1)}, bf16[32,64,128]{2,1,0:T(8,128)(2,1)S(1)}, u32[]{:S(2)}, u32[]{:S(2)}) %collective-permute-start.4) | collective-permute-done | bytes 524320 | tf_op jit(solution)/shard_map/ppermute | solution.py:284
  50.5 2.1 %collective-permute-start.5 = (bf16[32,64,128]{2,1,0:T(8,128)(2,1)S(1)}, bf16[32,64,128]{2,1,0:T(8,128)(2,1)S(1)}, u32[]{:S(2)}, u32[]{:S(2)}) collective-permute-start(bf16[32,64,128]{2,1,0:T(8,128)(2,1)S(1)} %broadcast_select_fusion.1), channel_id=1, source_target_pairs={{0,16},{4,12},{8,24},{12,4},{16,0},{20,28},{24,8},{28,20},{1,17},{... | collective-permute-start | bytes 1572872 | tf_op jit(solution)/shard_map/ppermute | solution.py:284
  52.6 0.8 fusion.10
  53.3 2.1 %collective-permute-done.12 = bf16[32,64,128]{2,1,0:T(8,128)(2,1)S(1)} collective-permute-done((bf16[32,64,128]{2,1,0:T(8,128)(2,1)S(1)}, bf16[32,64,128]{2,1,0:T(8,128)(2,1)S(1)}, u32[]{:S(2)}, u32[]{:S(2)}) %collective-permute-start.12) | collective-permute-done | bytes 524320 | tf_op jit(solution)/shard_map/ppermute | solution.py:284
  55.5 9.6 %collective-permute-start.13 = (bf16[32,64,128]{2,1,0:T(8,128)(2,1)S(1)}, bf16[32,64,128]{2,1,0:T(8,128)(2,1)S(1)}, u32[]{:S(2)}, u32[]{:S(2)}) collective-permute-start(bf16[32,64,128]{2,1,0:T(8,128)(2,1)S(1)} %broadcast_select_fusion.2.refs_0_), channel_id=1, source_target_pairs={{0,4},{4,0},{8,12},{12,8},{16,20},{20,16},{24,28},{28,24},{1,5},{5... | collective-permute-start | bytes 1572872 | tf_op jit(solution)/shard_map/ppermute | solution.py:291
  65.1 5.7 %collective-permute-start.6 = (bf16[32,64,128]{2,1,0:T(8,128)(2,1)S(1)}, bf16[32,64,128]{2,1,0:T(8,128)(2,1)S(1)}, u32[]{:S(2)}, u32[]{:S(2)}) collective-permute-start(bf16[32,64,128]{2,1,0:T(8,128)(2,1)S(1)} %broadcast_select_fusion.3.refs_0_), channel_id=1, source_target_pairs={{0,4},{4,0},{8,12},{12,8},{16,20},{20,16},{24,28},{28,24},{1,5},{5... | collective-permute-start | bytes 1572872 | tf_op jit(solution)/shard_map/ppermute | solution.py:291
  71.5 1.9 %add_add_fusion.own_ref = f32[4,128,128]{2,1,0:T(8,128)} fusion(f32[4,128,128]{2,1,0:T(8,128)} %collective-permute-done.2, f32[4,128,128]{2,1,0:T(8,128)} %collective-permute-done.1, f32[4,128,128]{2,1,0:T(8,128)S(1)} %collective-permute-done, f32[16,128,128]{2,1,0:T(8,128)} %correlate.3, s32[]{:T(128)S(6)} %select_n.136), kind=kLoop, calls=%fused_computation.9 | loop fusion | flops 196608 | bytes 1310724 | tf_op jit(solution)/shard_map/add | solution.py:250
  73.4 0.8 copy-done.3
  74.2 5.3 %correlate.5 = f32[16,64,128]{2,1,0:T(8,128)} custom-call(s32[2]{0:T(128)} %get-tuple-element.9.base_ref, bf16[32,64,128]{2,1,0:T(8,128)(2,1)} %copy-done.1, bf16[32,64,128]{2,1,0:T(8,128)(2,1)} %copy-done.3, bf16[128,64,128]{2,1,0:T(8,128)(2,1)} %get-tuple-element.7.refs_0_.refs_1_.refs_2_, bf16[128,64,128]{2,1,0:T(8,128)(2,1)} %get-tuple-element.8.refs_2_.refs_3_), custom_call_target="tpu_custom_call" | custom-call | flops 536870912 | bytes 5242880 | tf_op jit(solution)/shard_map/correlate/pallas_call | solution.py:181
  79.5 1.1 dynamic-slice_convert_fusion.2
  80.7 4.0 %collective-permute-start.15 = (f16[4,64,128]{2,1,0:T(8,128)(2,1)S(1)}, f16[4,64,128]{2,1,0:T(8,128)(2,1)S(1)}, u32[]{:S(2)}, u32[]{:S(2)}) collective-permute-start(f16[4,64,128]{2,1,0:T(8,128)(2,1)S(1)} %get-tuple-element.18), channel_id=1, source_target_pairs={{0,2},{1,3},{2,0},{3,1},{4,6},{5,7},{6,4},{7,5},{8,10},{9,11},{10,... | collective-permute-start | bytes 196616 | tf_op jit(solution)/shard_map/ppermute | solution.py:242
  85.1 0.8 copy-done.2
  85.9 5.3 %correlate.4 = f32[16,64,128]{2,1,0:T(8,128)} custom-call(s32[2]{0:T(128)} %get-tuple-element.10.base_ref, bf16[32,64,128]{2,1,0:T(8,128)(2,1)} %copy-done, bf16[32,64,128]{2,1,0:T(8,128)(2,1)} %copy-done.2, bf16[128,64,128]{2,1,0:T(8,128)(2,1)} %get-tuple-element.7.refs_0_.refs_1_.refs_2_, bf16[128,64,128]{2,1,0:T(8,128)(2,1)} %get-tuple-element.8.refs_2_.refs_3_), custom_call_target="tpu_custom_call" | custom-call | flops 536870912 | bytes 5242880 | tf_op jit(solution)/shard_map/correlate/pallas_call | solution.py:181
  91.2 1.1 dynamic-slice_convert_fusion.5
  92.5 3.8 %collective-permute-start.8 = (f16[4,64,128]{2,1,0:T(8,128)(2,1)S(1)}, f16[4,64,128]{2,1,0:T(8,128)(2,1)S(1)}, u32[]{:S(2)}, u32[]{:S(2)}) collective-permute-start(f16[4,64,128]{2,1,0:T(8,128)(2,1)S(1)} %get-tuple-element.21), channel_id=1, source_target_pairs={{0,2},{1,3},{2,0},{3,1},{4,6},{5,7},{6,4},{7,5},{8,10},{9,11},{10,... | collective-permute-start | bytes 196616 | tf_op jit(solution)/shard_map/ppermute | solution.py:242
  96.7 1.6 %convert_add_fusion.refs_1_ = f32[4,64,128]{2,1,0:T(8,128)} fusion(f16[4,64,128]{2,1,0:T(8,128)(2,1)S(1)} %collective-permute-done.16, f16[4,64,128]{2,1,0:T(8,128)(2,1)S(1)} %collective-permute-done.15, f16[4,64,128]{2,1,0:T(8,128)(2,1)S(1)} %collective-permute-done.14, f32[16,64,128]{2,1,0:T(8,128)} %correlate.5, s32[]{:T(128)S(6)} %select_n.136), kind=kLoop, calls=%fused_computation.16 | loop fusion | flops 196608 | bytes 458756 | tf_op jit(solution)/shard_map/add | solution.py:250
  98.3 2.0 %collective-permute-done.8 = f16[4,64,128]{2,1,0:T(8,128)(2,1)S(1)} collective-permute-done((f16[4,64,128]{2,1,0:T(8,128)(2,1)S(1)}, f16[4,64,128]{2,1,0:T(8,128)(2,1)S(1)}, u32[]{:S(2)}, u32[]{:S(2)}) %collective-permute-start.8) | collective-permute-done | bytes 65568 | tf_op jit(solution)/shard_map/ppermute | solution.py:242
  100.3 2.1 %collective-permute-done.9 = f16[4,64,128]{2,1,0:T(8,128)(2,1)S(1)} collective-permute-done((f16[4,64,128]{2,1,0:T(8,128)(2,1)S(1)}, f16[4,64,128]{2,1,0:T(8,128)(2,1)S(1)}, u32[]{:S(2)}, u32[]{:S(2)}) %collective-permute-start.9) | collective-permute-done | bytes 65568 | tf_op jit(solution)/shard_map/ppermute | solution.py:242
  102.4 1.6 %convert_add_fusion.1.refs_0_ = f32[4,64,128]{2,1,0:T(8,128)} fusion(f16[4,64,128]{2,1,0:T(8,128)(2,1)S(1)} %collective-permute-done.9, f16[4,64,128]{2,1,0:T(8,128)(2,1)S(1)} %collective-permute-done.8, f16[4,64,128]{2,1,0:T(8,128)(2,1)S(1)} %collective-permute-done.7, f32[16,64,128]{2,1,0:T(8,128)} %correlate.4, s32[]{:T(128)S(6)} %select_n.136), kind=kLoop, calls=%fused_computation.20 | loop fusion | flops 196608 | bytes 458756 | tf_op jit(solution)/shard_map/add | solution.py:250
  104.7 2.1 %finish.1 = f32[2,4,2,16,512]{4,3,2,1,0:T(8,128)} custom-call(s32[2]{0:T(128)} %pad_add_fusion.sel_ref, f32[2,4,16,128]{3,2,1,0:T(8,128)} %broadcast_in_dim.12.keep_ref, f32[4,128,128]{2,1,0:T(8,128)} %add_add_fusion.own_ref, f32[4,64,128]{2,1,0:T(8,128)} %convert_add_fusion.1.refs_0_, f32[4,64,128]{2,1,0:T(8,128)} %convert_add_fusion.refs_1_), custom_call_target="tpu_custom_call" | custom-call | tf_op jit(solution)/shard_map/finish/pallas_call | solution.py:224
  (40 shorter events, 5.4 us)
Async XLA Ops:
  1.6 15.8 %copy-start.4 = (s32[2]{0:T(128)S(1)}, s32[2]{0:T(128)}, u32[]{:S(2)}) copy-start(s32[2]{0:T(128)} %param.4) | copy-start | bytes 28
  16.9 2.9 %collective-permute-start.10 = (bf16[32,64,128]{2,1,0:T(8,128)(2,1)S(1)}, bf16[32,64,128]{2,1,0:T(8,128)(2,1)S(1)}, u32[]{:S(2)}, u32[]{:S(2)}) collective-permute-start(bf16[32,64,128]{2,1,0:T(8,128)(2,1)S(1)} %constant_dynamic-slice_fusion), channel_id=1, source_target_pairs={{0,4},{4,0},{8,12},{12,8},{16,20},{20,16},{24,28},{28,24},{1,5},{5... | collective-permute-start | bytes 1572872 | tf_op jit(solution)/shard_map/ppermute | solution.py:277
  21.1 16.5 %collective-permute-start.3 = (bf16[32,64,128]{2,1,0:T(8,128)(2,1)S(1)}, bf16[32,64,128]{2,1,0:T(8,128)(2,1)S(1)}, u32[]{:S(2)}, u32[]{:S(2)}) collective-permute-start(bf16[32,64,128]{2,1,0:T(8,128)(2,1)S(1)} %get-tuple-element.12), channel_id=1, source_target_pairs={{0,4},{4,0},{8,12},{12,8},{16,20},{20,16},{24,28},{28,24},{1,5},{5... | collective-permute-start | bytes 1572872 | tf_op jit(solution)/shard_map/ppermute | solution.py:277
  31.3 40.2 %collective-permute-start = (f32[4,128,128]{2,1,0:T(8,128)}, f32[4,128,128]{2,1,0:T(8,128)S(1)}, u32[]{:S(2)}, u32[]{:S(2)}) collective-permute-start(f32[4,128,128]{2,1,0:T(8,128)} %get-tuple-element.13), channel_id=1, source_target_pairs={{28,29},{29,28},{30,31},{31,30}} | collective-permute-start | bytes 786440 | tf_op jit(solution)/shard_map/ppermute | solution.py:246
  32.0 39.5 %collective-permute-start.1 = (f32[4,128,128]{2,1,0:T(8,128)}, f32[4,128,128]{2,1,0:T(8,128)}, u32[]{:S(2)}, u32[]{:S(2)}) collective-permute-start(f32[4,128,128]{2,1,0:T(8,128)} %get-tuple-element.15), channel_id=1, source_target_pairs={{28,30},{29,31},{30,28},{31,29}} | collective-permute-start | bytes 786440 | tf_op jit(solution)/shard_map/ppermute | solution.py:246
  33.4 38.2 %collective-permute-start.2 = (f32[4,128,128]{2,1,0:T(8,128)}, f32[4,128,128]{2,1,0:T(8,128)}, u32[]{:S(2)}, u32[]{:S(2)}) collective-permute-start(f32[4,128,128]{2,1,0:T(8,128)} %get-tuple-element.14), channel_id=1, source_target_pairs={{28,31},{29,30},{30,29},{31,28}} | collective-permute-start | bytes 786440 | tf_op jit(solution)/shard_map/ppermute | solution.py:246
  34.7 10.1 %collective-permute-start.11 = (bf16[32,64,128]{2,1,0:T(8,128)(2,1)S(1)}, bf16[32,64,128]{2,1,0:T(8,128)(2,1)S(1)}, u32[]{:S(2)}, u32[]{:S(2)}) collective-permute-start(bf16[32,64,128]{2,1,0:T(8,128)(2,1)S(1)} %get-tuple-element.11), channel_id=1, source_target_pairs={{0,8},{4,20},{8,0},{12,28},{16,24},{20,4},{24,16},{28,12},{1,9},{5... | collective-permute-start | bytes 1572872 | tf_op jit(solution)/shard_map/ppermute | solution.py:284
  38.7 11.7 %collective-permute-start.4 = (bf16[32,64,128]{2,1,0:T(8,128)(2,1)S(1)}, bf16[32,64,128]{2,1,0:T(8,128)(2,1)S(1)}, u32[]{:S(2)}, u32[]{:S(2)}) collective-permute-start(bf16[32,64,128]{2,1,0:T(8,128)(2,1)S(1)} %dynamic-slice_select_fusion.1), channel_id=1, source_target_pairs={{0,8},{4,20},{8,0},{12,28},{16,24},{20,4},{24,16},{28,12},{1,9},{5... | collective-permute-start | bytes 1572872 | tf_op jit(solution)/shard_map/ppermute | solution.py:284
  44.8 10.6 %collective-permute-start.12 = (bf16[32,64,128]{2,1,0:T(8,128)(2,1)S(1)}, bf16[32,64,128]{2,1,0:T(8,128)(2,1)S(1)}, u32[]{:S(2)}, u32[]{:S(2)}) collective-permute-start(bf16[32,64,128]{2,1,0:T(8,128)(2,1)S(1)} %broadcast_select_fusion), channel_id=1, source_target_pairs={{0,16},{4,12},{8,24},{12,4},{16,0},{20,28},{24,8},{28,20},{1,17},{... | collective-permute-start | bytes 1572872 | tf_op jit(solution)/shard_map/ppermute | solution.py:284
  50.5 14.6 %collective-permute-start.5 = (bf16[32,64,128]{2,1,0:T(8,128)(2,1)S(1)}, bf16[32,64,128]{2,1,0:T(8,128)(2,1)S(1)}, u32[]{:S(2)}, u32[]{:S(2)}) collective-permute-start(bf16[32,64,128]{2,1,0:T(8,128)(2,1)S(1)} %broadcast_select_fusion.1), channel_id=1, source_target_pairs={{0,16},{4,12},{8,24},{12,4},{16,0},{20,28},{24,8},{28,20},{1,17},{... | collective-permute-start | bytes 1572872 | tf_op jit(solution)/shard_map/ppermute | solution.py:284
  55.5 17.9 %copy-start.1 = (bf16[32,64,128]{2,1,0:T(8,128)(2,1)}, bf16[32,64,128]{2,1,0:T(8,128)(2,1)S(1)}, u32[]{:S(2)}) copy-start(bf16[32,64,128]{2,1,0:T(8,128)(2,1)S(1)} %broadcast_select_fusion.2.refs_0_) | copy-start | bytes 1572868
  55.5 17.9 %collective-permute-start.13 = (bf16[32,64,128]{2,1,0:T(8,128)(2,1)S(1)}, bf16[32,64,128]{2,1,0:T(8,128)(2,1)S(1)}, u32[]{:S(2)}, u32[]{:S(2)}) collective-permute-start(bf16[32,64,128]{2,1,0:T(8,128)(2,1)S(1)} %broadcast_select_fusion.2.refs_0_), channel_id=1, source_target_pairs={{0,4},{4,0},{8,12},{12,8},{16,20},{20,16},{24,28},{28,24},{1,5},{5... | collective-permute-start | bytes 1572872 | tf_op jit(solution)/shard_map/ppermute | solution.py:291
  65.1 14.4 %copy-start = (bf16[32,64,128]{2,1,0:T(8,128)(2,1)}, bf16[32,64,128]{2,1,0:T(8,128)(2,1)S(1)}, u32[]{:S(2)}) copy-start(bf16[32,64,128]{2,1,0:T(8,128)(2,1)S(1)} %broadcast_select_fusion.3.refs_0_) | copy-start | bytes 1572868
  65.1 19.9 %collective-permute-start.6 = (bf16[32,64,128]{2,1,0:T(8,128)(2,1)S(1)}, bf16[32,64,128]{2,1,0:T(8,128)(2,1)S(1)}, u32[]{:S(2)}, u32[]{:S(2)}) collective-permute-start(bf16[32,64,128]{2,1,0:T(8,128)(2,1)S(1)} %broadcast_select_fusion.3.refs_0_), channel_id=1, source_target_pairs={{0,4},{4,0},{8,12},{12,8},{16,20},{20,16},{24,28},{28,24},{1,5},{5... | collective-permute-start | bytes 1572872 | tf_op jit(solution)/shard_map/ppermute | solution.py:291
  73.4 0.8 copy-start.3
  80.6 15.8 %collective-permute-start.14 = (f16[4,64,128]{2,1,0:T(8,128)(2,1)S(1)}, f16[4,64,128]{2,1,0:T(8,128)(2,1)S(1)}, u32[]{:S(2)}, u32[]{:S(2)}) collective-permute-start(f16[4,64,128]{2,1,0:T(8,128)(2,1)S(1)} %get-tuple-element.16), channel_id=1, source_target_pairs={{0,1},{1,0},{2,3},{3,2},{4,5},{5,4},{6,7},{7,6},{8,9},{9,8},{10,11... | collective-permute-start | bytes 196616 | tf_op jit(solution)/shard_map/ppermute | solution.py:242
  80.7 16.0 %collective-permute-start.15 = (f16[4,64,128]{2,1,0:T(8,128)(2,1)S(1)}, f16[4,64,128]{2,1,0:T(8,128)(2,1)S(1)}, u32[]{:S(2)}, u32[]{:S(2)}) collective-permute-start(f16[4,64,128]{2,1,0:T(8,128)(2,1)S(1)} %get-tuple-element.18), channel_id=1, source_target_pairs={{0,2},{1,3},{2,0},{3,1},{4,6},{5,7},{6,4},{7,5},{8,10},{9,11},{10,... | collective-permute-start | bytes 196616 | tf_op jit(solution)/shard_map/ppermute | solution.py:242
  84.7 12.0 %collective-permute-start.16 = (f16[4,64,128]{2,1,0:T(8,128)(2,1)S(1)}, f16[4,64,128]{2,1,0:T(8,128)(2,1)S(1)}, u32[]{:S(2)}, u32[]{:S(2)}) collective-permute-start(f16[4,64,128]{2,1,0:T(8,128)(2,1)S(1)} %get-tuple-element.17), channel_id=1, source_target_pairs={{0,3},{1,2},{2,1},{3,0},{4,7},{5,6},{6,5},{7,4},{8,11},{9,10},{10,... | collective-permute-start | bytes 196616 | tf_op jit(solution)/shard_map/ppermute | solution.py:242
  85.1 0.8 copy-start.2
  92.3 6.1 %collective-permute-start.7 = (f16[4,64,128]{2,1,0:T(8,128)(2,1)S(1)}, f16[4,64,128]{2,1,0:T(8,128)(2,1)S(1)}, u32[]{:S(2)}, u32[]{:S(2)}) collective-permute-start(f16[4,64,128]{2,1,0:T(8,128)(2,1)S(1)} %get-tuple-element.19), channel_id=1, source_target_pairs={{0,1},{1,0},{2,3},{3,2},{4,5},{5,4},{6,7},{7,6},{8,9},{9,8},{10,11... | collective-permute-start | bytes 196616 | tf_op jit(solution)/shard_map/ppermute | solution.py:242
  92.5 7.8 %collective-permute-start.8 = (f16[4,64,128]{2,1,0:T(8,128)(2,1)S(1)}, f16[4,64,128]{2,1,0:T(8,128)(2,1)S(1)}, u32[]{:S(2)}, u32[]{:S(2)}) collective-permute-start(f16[4,64,128]{2,1,0:T(8,128)(2,1)S(1)} %get-tuple-element.21), channel_id=1, source_target_pairs={{0,2},{1,3},{2,0},{3,1},{4,6},{5,7},{6,4},{7,5},{8,10},{9,11},{10,... | collective-permute-start | bytes 196616 | tf_op jit(solution)/shard_map/ppermute | solution.py:242
  96.4 6.1 %collective-permute-start.9 = (f16[4,64,128]{2,1,0:T(8,128)(2,1)S(1)}, f16[4,64,128]{2,1,0:T(8,128)(2,1)S(1)}, u32[]{:S(2)}, u32[]{:S(2)}) collective-permute-start(f16[4,64,128]{2,1,0:T(8,128)(2,1)S(1)} %get-tuple-element.20), channel_id=1, source_target_pairs={{0,3},{1,2},{2,1},{3,0},{4,7},{5,6},{6,5},{7,4},{8,11},{9,10},{10,... | collective-permute-start | bytes 196616 | tf_op jit(solution)/shard_map/ppermute | solution.py:242
